TPU v7x, 32 devices: a whole 2x2x4 slice. The times are simulated.
32 devices in a mesh: band: 16 (over z, x, core), dom: 2 (over y).
Axes of the slice: x: 2, y: 2, z: 4, core: 2. Of those that a mesh axis runs over, the one named last changes fastest.
Arguments:
- orbitals: bfloat16 [128, 64, 32, 128], P('band', None, 'dom'), may hold values from -6 to 6
- occupations: float32 [128], P('band'), may hold values from 0.25 to 2
Outputs:
- potential: float32 [128, 64, 256], P('band', 'dom')
All inputs are finite; a program needn't handle non-finite values.
Results may differ from a plain program's by a relative error of at most 0.0003.
Values sent between devices are 32-bit elements; how exact they have to be, the bound alone decides.
No kernel may reach another device: no remote copies, remote signals or barrier semaphores. Data moves between devices by JAX's collectives and lax.ppermute only.
A program may use at most 64 MiB of HBM per device.

v0:
```python
import jax
import jax.numpy as jnp
from jax import lax
from jax.sharding import PartitionSpec as P

interp_weights = (
    3.0 / 256.0,
    -25.0 / 256.0,
    150.0 / 256.0,
    150.0 / 256.0,
    -25.0 / 256.0,
    3.0 / 256.0,
)
deriv_factors = (4.0 / 5.0, -1.0 / 5.0, 4.0 / 105.0, -1.0 / 280.0)


def padded_2(value, sides, width):
    for axis, dim in sides:
        devices, length = (lax.axis_size(axis), value.shape[dim])
        up = [(i, (i + 1) % devices) for i in range(devices)]
        down = [(j, i) for i, j in up]
        last = lax.slice_in_dim(value, length - width, length, axis=dim)
        initial = lax.slice_in_dim(value, 0, width, axis=dim)
        before = lax.ppermute(last, axis, up)
        after = lax.ppermute(initial, axis, down)
        value = jnp.concatenate([before, value, after], axis=dim)
    return value


def alternate(even_cells, odd_cells, along):
    stacked = jnp.stack([even_cells, odd_cells], axis=along + 1)
    target_shape = list(even_cells.shape)
    target_shape[along] = 2 * even_cells.shape[along]
    return stacked.reshape(target_shape)


def refine(padded, along, extent):
    odd_cells = jnp.zeros_like(lax.slice_in_dim(padded, 3, 3 + extent, axis=along))
    for offset, factor in zip(range(-2, 4), interp_weights):
        odd_cells = odd_cells + factor * lax.slice_in_dim(
            padded, 3 + offset, 3 + offset + extent, axis=along
        )
    even_cells = lax.slice_in_dim(padded, 3, 3 + extent, axis=along)
    return alternate(even_cells, odd_cells, along)


def wrap_third(field, margin):
    extent = field.shape[2]
    return jnp.concatenate([field[:, :, extent - margin :], field, field[:, :, :margin]], axis=2)


def central(padded, along, start_a, start_b, extent_a, extent_b):
    window_base = padded[start_a : start_a + extent_a, start_b : start_b + extent_b]
    summed = jnp.zeros_like(window_base)
    for offset, factor in zip((1, 2, 3, 4), deriv_factors):
        if along == 0:
            ahead_part = padded[
                start_a + offset : start_a + offset + extent_a, start_b : start_b + extent_b
            ]
            behind_part = padded[
                start_a - offset : start_a - offset + extent_a, start_b : start_b + extent_b
            ]
        elif along == 1:
            ahead_part = padded[
                start_a : start_a + extent_a, start_b + offset : start_b + offset + extent_b
            ]
            behind_part = padded[
                start_a : start_a + extent_a, start_b - offset : start_b - offset + extent_b
            ]
        else:
            ahead_part = jnp.roll(window_base, -offset, 2)
            behind_part = jnp.roll(window_base, offset, 2)
        summed = summed + factor * (ahead_part - behind_part)
    return summed


def pointwise(density, grad_a, grad_b, grad_c):
    shifted = density * density + 0.01
    scaling = 0.01 * shifted ** (4.0 / 3.0)
    reduced = (grad_a * grad_a + grad_b * grad_b + grad_c * grad_c) / scaling
    divisor = 1.0 + 0.2195 * reduced / 0.804
    enhance = 0.804 - 0.804 / divisor
    flux_weight = 0.2195 / (divisor * divisor) / scaling
    local_part = -0.75 * shifted ** (1.0 / 6.0) * (1.0 + enhance)
    return (local_part, flux_weight * grad_a, flux_weight * grad_b, flux_weight * grad_c)


def deep_tail(deep, extent_a, extent_b):
    wider_a, wider_b = (extent_a + 8, extent_b + 8)
    grad_a = central(deep, 0, 4, 4, wider_a, wider_b)
    grad_b = central(deep, 1, 4, 4, wider_a, wider_b)
    grad_c = central(deep, 2, 4, 4, wider_a, wider_b)
    local_part, flux_a, flux_b, flux_c = pointwise(
        deep[4 : 4 + wider_a, 4 : 4 + wider_b], grad_a, grad_b, grad_c
    )
    div_a = central(flux_a, 0, 4, 4, extent_a, extent_b)
    div_b = central(flux_b, 1, 4, 4, extent_a, extent_b)
    div_c = central(flux_c, 2, 4, 4, extent_a, extent_b)
    local_part = local_part[4 : 4 + extent_a, 4 : 4 + extent_b]
    return local_part + 0.2 * (div_a + div_b + div_c)


def on_device(orbitals, occupations):
    weights = occupations / (occupations.shape[0] * lax.axis_size("band"))
    density = lax.psum_scatter(
        jnp.sum(weights[:, None, None, None] * jnp.square(orbitals.astype(jnp.float32)), axis=0),
        "band",
        scatter_dimension=0,
        tiled=True,
    )
    cells_a, cells_b = (density.shape[0], density.shape[1])
    padded = padded_2(density, (("band", 0), ("dom", 1)), 3)
    extent_a, extent_b = (2 * cells_a, 2 * cells_b)
    fine = refine(padded, 0, cells_a)
    fine = refine(fine, 1, cells_b)
    fine = refine(wrap_third(fine, 3), 2, density.shape[2])
    deep = padded_2(fine, (("band", 0), ("dom", 1)), 8)
    return deep_tail(deep, extent_a, extent_b)


def solution(mesh):
    return jax.shard_map(
        on_device,
        mesh=mesh,
        in_specs=(P("band", None, "dom", None), P("band")),
        out_specs=P("band", "dom", None),
        check_vma=False,
    )
```

profile of v0, /device:TPU:0, one launch (start us, length us, event | category | flops | bytes accessed | tf_op | source)
XLA Modules:
  0.0 118.9 jit_solution(3710449548425866962)
XLA Ops:
  6.5 0.7 broadcast_multiply_fusion
  7.2 3.0 %multiply_reduce_fusion = f32[64,16,128]{2,1,0:T(8,128)} fusion(bf16[8,64,16,128]{3,2,1,0:T(8,128)(2,1)} %param.2, f32[8]{0:T(128)S(1)} %broadcast_multiply_fusion), kind=kLoop, calls=%fused_computation | loop fusion | flops 4063232 | bytes 2621472 | tf_op jit(solution)/shard_map/reduce_sum | solution.py:106
  10.2 59.5 %reduce-scatter.2.cloned.1.call-done = f32[4,16,128]{2,1,0:T(8,128)} async-done(((f32[64,16,128]{2,1,0:T(8,128)}), f32[4,16,128]{2,1,0:T(8,128)}) %reduce-scatter.2.cloned.1.call-update) | async-done | bytes 32784 | tf_op jit(solution)/shard_map/reduce_scatter | solution.py:105
  69.8 0.8 fusion.100
  70.6 4.4 %collective-permute-start.1 = (f32[3,16,128]{2,1,0:T(8,128)S(1)}, f32[3,16,128]{2,1,0:T(8,128)S(1)}, u32[]{:S(2)}, u32[]{:S(2)}) collective-permute-start(f32[3,16,128]{2,1,0:T(8,128)S(1)} %get-tuple-element.54), channel_id=1, source_target_pairs={{2,0},{4,2},{6,4},{8,6},{10,8},{12,10},{14,12},{16,14},{18,16},{20... | collective-permute-start | bytes 73736 | tf_op jit(solution)/shard_map/ppermute | solution.py:25
  75.0 1.5 %collective-permute-done = f32[3,16,128]{2,1,0:T(8,128)S(1)} collective-permute-done((f32[3,16,128]{2,1,0:T(8,128)S(1)}, f32[3,16,128]{2,1,0:T(8,128)S(1)}, u32[]{:S(2)}, u32[]{:S(2)}) %collective-permute-start) | collective-permute-done | bytes 24608 | tf_op jit(solution)/shard_map/ppermute | solution.py:24
  76.5 0.8 constant_dynamic-update-slice_fusion.1
  77.3 1.5 %collective-permute-start.2 = (f32[10,3,128]{2,1,0:T(4,128)S(1)}, f32[10,3,128]{2,1,0:T(4,128)S(1)}, u32[]{:S(2)}, u32[]{:S(2)}) collective-permute-start(f32[10,3,128]{2,1,0:T(4,128)S(1)} %get-tuple-element.52), channel_id=1, source_target_pairs={{0,1},{1,0},{2,3},{3,2},{4,5},{5,4},{6,7},{7,6},{8,9},{9,8},{10,11... | collective-permute-start | bytes 46088 | tf_op jit(solution)/shard_map/ppermute | solution.py:24
  78.9 0.6 collective-permute-start.3
  79.4 1.8 %collective-permute-done.2 = f32[10,3,128]{2,1,0:T(4,128)S(1)} collective-permute-done((f32[10,3,128]{2,1,0:T(4,128)S(1)}, f32[10,3,128]{2,1,0:T(4,128)S(1)}, u32[]{:S(2)}, u32[]{:S(2)}) %collective-permute-start.2) | collective-permute-done | bytes 15392 | tf_op jit(solution)/shard_map/ppermute | solution.py:24
  81.2 1.5 %collective-permute-done.3 = f32[10,3,128]{2,1,0:T(4,128)S(1)} collective-permute-done((f32[10,3,128]{2,1,0:T(4,128)S(1)}, f32[10,3,128]{2,1,0:T(4,128)S(1)}, u32[]{:S(2)}, u32[]{:S(2)}) %collective-permute-start.3) | collective-permute-done | bytes 15392 | tf_op jit(solution)/shard_map/ppermute | solution.py:25
  83.0 0.4 fusion.58
  83.5 0.5 copy.23
  84.0 0.4 copy.24
  84.4 2.3 %collective-permute-start.5 = (f32[8,32,256]{2,1,0:T(8,128)S(1)}, f32[8,32,256]{2,1,0:T(8,128)S(1)}, u32[]{:S(2)}, u32[]{:S(2)}) collective-permute-start(f32[8,32,256]{2,1,0:T(8,128)S(1)} %copy.24), channel_id=1, source_target_pairs={{2,0},{4,2},{6,4},{8,6},{10,8},{12,10},{14,12},{16,14},{18,16},{20... | collective-permute-start | bytes 786440 | tf_op jit(solution)/shard_map/ppermute | solution.py:25
  86.7 3.9 %collective-permute-done.5 = f32[8,32,256]{2,1,0:T(8,128)S(1)} collective-permute-done((f32[8,32,256]{2,1,0:T(8,128)S(1)}, f32[8,32,256]{2,1,0:T(8,128)S(1)}, u32[]{:S(2)}, u32[]{:S(2)}) %collective-permute-start.5) | collective-permute-done | bytes 262176 | tf_op jit(solution)/shard_map/ppermute | solution.py:25
  90.5 4.6 %collective-permute-done.4 = f32[8,32,256]{2,1,0:T(8,128)S(1)} collective-permute-done((f32[8,32,256]{2,1,0:T(8,128)S(1)}, f32[8,32,256]{2,1,0:T(8,128)S(1)}, u32[]{:S(2)}, u32[]{:S(2)}) %collective-permute-start.4) | collective-permute-done | bytes 262176 | tf_op jit(solution)/shard_map/ppermute | solution.py:24
  95.2 0.6 collective-permute-start.6
  95.8 1.5 %collective-permute-start.7 = (f32[24,8,256]{2,1,0:T(8,128)S(1)}, f32[24,8,256]{2,1,0:T(8,128)S(1)}, u32[]{:S(2)}, u32[]{:S(2)}) collective-permute-start(f32[24,8,256]{2,1,0:T(8,128)S(1)} %get-tuple-element.29), channel_id=1, source_target_pairs={{1,0},{0,1},{3,2},{2,3},{5,4},{4,5},{7,6},{6,7},{9,8},{8,9},{11,10... | collective-permute-start | bytes 589832 | tf_op jit(solution)/shard_map/ppermute | solution.py:25
  97.3 3.6 %collective-permute-done.6 = f32[24,8,256]{2,1,0:T(8,128)S(1)} collective-permute-done((f32[24,8,256]{2,1,0:T(8,128)S(1)}, f32[24,8,256]{2,1,0:T(8,128)S(1)}, u32[]{:S(2)}, u32[]{:S(2)}) %collective-permute-start.6) | collective-permute-done | bytes 196640 | tf_op jit(solution)/shard_map/ppermute | solution.py:24
  100.9 2.1 %collective-permute-done.7 = f32[24,8,256]{2,1,0:T(8,128)S(1)} collective-permute-done((f32[24,8,256]{2,1,0:T(8,128)S(1)}, f32[24,8,256]{2,1,0:T(8,128)S(1)}, u32[]{:S(2)}, u32[]{:S(2)}) %collective-permute-start.7) | collective-permute-done | bytes 196640 | tf_op jit(solution)/shard_map/ppermute | solution.py:25
  104.8 3.7 %fusion.77 = (f32[16,40,256]{2,1,0:T(8,128)S(1)}, f32[16,40,256]{2,1,0:T(8,128)S(1)}, f32[16,40,256]{2,1,0:T(8,128)S(1)}, f32[16,40,256]{2,1,0:T(8,128)S(1)}) fusion(f32[24,48,256]{2,1,0:T(8,128)S(1)} %pad_maximum_fusion, f32[8,32,256]{2,1,0:T(8,128)S(1)} %collective-permute-done.5, f32[8,32,256]{2,1,0:T(8,128)S(1)} %copy.24, ...), kind=kLoop, calls=%fused_computation.145 | loop fusion | flops 10158080 | bytes 18874368 | tf_op jit(solution)/shard_map/mul | solution.py:85
  109.5 0.9 fusion.79
  110.4 1.7 %fusion.28 = f32[8,32,256]{2,1,0:T(8,128)} fusion(f32[16,40,256]{2,1,0:T(8,128)S(1)} %get-tuple-element.10, f32[16,40,256]{2,1,0:T(8,128)S(1)} %get-tuple-element.9, f32[16,40,256]{2,1,0:T(8,128)S(1)} %get-tuple-element.6, f32[16,40,256]{2,1,0:T(8,128)S(1)} %get-tuple-element.11, f32[8,32,1]{2,1,0:T(8,128)S(1)} %get-tuple-element.43, ...), kind=kLoop, calls=%fused_computation.56 | loop fusion | flops 3211264 | bytes 7077888 | tf_op jit(solution)/shard_map/add | solution.py:100
  (36 shorter events, 3.1 us)
Async XLA Ops:
  6.5 63.2 %reduce-scatter.2.cloned.1.call-start = ((), (), s32[]{:S(2)}) async-start(), calls=%async_computation.1 | async-start | bytes 557056 | tf_op jit(solution)/shard_map/reduce_scatter | solution.py:105
  70.6 5.9 %collective-permute-start = (f32[3,16,128]{2,1,0:T(8,128)S(1)}, f32[3,16,128]{2,1,0:T(8,128)S(1)}, u32[]{:S(2)}, u32[]{:S(2)}) collective-permute-start(f32[3,16,128]{2,1,0:T(8,128)S(1)} %get-tuple-element.55), channel_id=1, source_target_pairs={{0,2},{2,4},{4,6},{6,8},{8,10},{10,12},{12,14},{14,16},{16,18},{18... | collective-permute-start | bytes 73736 | tf_op jit(solution)/shard_map/ppermute | solution.py:24
  70.6 6.7 %collective-permute-start.1 = (f32[3,16,128]{2,1,0:T(8,128)S(1)}, f32[3,16,128]{2,1,0:T(8,128)S(1)}, u32[]{:S(2)}, u32[]{:S(2)}) collective-permute-start(f32[3,16,128]{2,1,0:T(8,128)S(1)} %get-tuple-element.54), channel_id=1, source_target_pairs={{2,0},{4,2},{6,4},{8,6},{10,8},{12,10},{14,12},{16,14},{18,16},{20... | collective-permute-start | bytes 73736 | tf_op jit(solution)/shard_map/ppermute | solution.py:25
  77.3 3.8 %collective-permute-start.2 = (f32[10,3,128]{2,1,0:T(4,128)S(1)}, f32[10,3,128]{2,1,0:T(4,128)S(1)}, u32[]{:S(2)}, u32[]{:S(2)}) collective-permute-start(f32[10,3,128]{2,1,0:T(4,128)S(1)} %get-tuple-element.52), channel_id=1, source_target_pairs={{0,1},{1,0},{2,3},{3,2},{4,5},{5,4},{6,7},{7,6},{8,9},{9,8},{10,11... | collective-permute-start | bytes 46088 | tf_op jit(solution)/shard_map/ppermute | solution.py:24
  78.9 3.8 %collective-permute-start.3 = (f32[10,3,128]{2,1,0:T(4,128)S(1)}, f32[10,3,128]{2,1,0:T(4,128)S(1)}, u32[]{:S(2)}, u32[]{:S(2)}) collective-permute-start(f32[10,3,128]{2,1,0:T(4,128)S(1)} %get-tuple-element.53), channel_id=1, source_target_pairs={{1,0},{0,1},{3,2},{2,3},{5,4},{4,5},{7,6},{6,7},{9,8},{8,9},{11,10... | collective-permute-start | bytes 46088 | tf_op jit(solution)/shard_map/ppermute | solution.py:25
  84.4 6.2 %collective-permute-start.5 = (f32[8,32,256]{2,1,0:T(8,128)S(1)}, f32[8,32,256]{2,1,0:T(8,128)S(1)}, u32[]{:S(2)}, u32[]{:S(2)}) collective-permute-start(f32[8,32,256]{2,1,0:T(8,128)S(1)} %copy.24), channel_id=1, source_target_pairs={{2,0},{4,2},{6,4},{8,6},{10,8},{12,10},{14,12},{16,14},{18,16},{20... | collective-permute-start | bytes 786440 | tf_op jit(solution)/shard_map/ppermute | solution.py:25
  86.7 8.5 %collective-permute-start.4 = (f32[8,32,256]{2,1,0:T(8,128)S(1)}, f32[8,32,256]{2,1,0:T(8,128)S(1)}, u32[]{:S(2)}, u32[]{:S(2)}) collective-permute-start(f32[8,32,256]{2,1,0:T(8,128)S(1)} %copy.24), channel_id=1, source_target_pairs={{0,2},{2,4},{4,6},{6,8},{8,10},{10,12},{12,14},{14,16},{16,18},{18... | collective-permute-start | bytes 786440 | tf_op jit(solution)/shard_map/ppermute | solution.py:24
  95.2 5.7 %collective-permute-start.6 = (f32[24,8,256]{2,1,0:T(8,128)S(1)}, f32[24,8,256]{2,1,0:T(8,128)S(1)}, u32[]{:S(2)}, u32[]{:S(2)}) collective-permute-start(f32[24,8,256]{2,1,0:T(8,128)S(1)} %get-tuple-element.28), channel_id=1, source_target_pairs={{0,1},{1,0},{2,3},{3,2},{4,5},{5,4},{6,7},{7,6},{8,9},{9,8},{10,11... | collective-permute-start | bytes 589832 | tf_op jit(solution)/shard_map/ppermute | solution.py:24
  95.8 7.2 %collective-permute-start.7 = (f32[24,8,256]{2,1,0:T(8,128)S(1)}, f32[24,8,256]{2,1,0:T(8,128)S(1)}, u32[]{:S(2)}, u32[]{:S(2)}) collective-permute-start(f32[24,8,256]{2,1,0:T(8,128)S(1)} %get-tuple-element.29), channel_id=1, source_target_pairs={{1,0},{0,1},{3,2},{2,3},{5,4},{4,5},{7,6},{6,7},{9,8},{8,9},{11,10... | collective-permute-start | bytes 589832 | tf_op jit(solution)/shard_map/ppermute | solution.py:25
Sparse Core Ops, SparseCore 0:
  10.9 58.8 reduce-scatter.1
where the time goes:
time: 119 us
  waiting for transfers between devices  78.5 us (66%)
  between operations  13.6 us (11%)
  starting transfers between devices  10.9 us (9%)
  other arithmetic  10.6 us (9%)
  local copies, waits for them, and re-layouts  5.29 us (4%)
    reduce_scatter x1, waiting for transfers between devices, on_device(): lax.psum_scatter(jnp.sum(weights[:, None, None, None] * jnp.square(orbita...  59.5 us
    ppermute x4, waiting for transfers between devices, padded_2(): before = lax.ppermute(last, axis, up)  11.5 us
    ppermute x4, starting transfers between devices, padded_2(): after = lax.ppermute(initial, axis, down)  8.74 us
    ppermute x4, waiting for transfers between devices, padded_2(): after = lax.ppermute(initial, axis, down)  7.45 us
    mul x1, other arithmetic, pointwise(): flux_weight * grad_c  3.71 us
    reduce_sum x1, other arithmetic, on_device(): jnp.sum(weights[:, None, None, None] * jnp.square(orbitals.astype(jnp.flo...  3.02 us
    slice x16, local copies, waits for them, and re-layouts, central(): behind_part = jnp.roll(window_base, offset, 2)  2.56 us
  transfers between devices with their start and end apart: 9, of which 8 were waited for; matrix products, arithmetic and copies ran while one was open for 1% of the time, Pallas kernels for 0%

commit v1 on v0

v1 whole, which is shorter than its diff:
```python
import functools

import jax
import jax.numpy as jnp
import numpy as np
from jax import lax
from jax.experimental import pallas as pl
from jax.experimental.pallas import tpu as pltpu
from jax.sharding import PartitionSpec as P

interp_weights = (
    3.0 / 256.0,
    -25.0 / 256.0,
    150.0 / 256.0,
    150.0 / 256.0,
    -25.0 / 256.0,
    3.0 / 256.0,
)
deriv_factors = (4.0 / 5.0, -1.0 / 5.0, 4.0 / 105.0, -1.0 / 280.0)
BEFORE, AFTER = 6, 7
SIDE = 8
HIGHEST = lax.Precision.HIGHEST


def third_matrices(cells):
    refine = np.zeros((cells, 2 * cells))
    for i in range(cells):
        refine[i, 2 * i] = 1.0
        for offset, factor in zip(range(-2, 4), interp_weights):
            refine[(i + offset) % cells, 2 * i + 1] += factor
    derive = np.zeros((2 * cells, 2 * cells))
    for i in range(2 * cells):
        for offset, factor in zip((1, 2, 3, 4), deriv_factors):
            derive[(i + offset) % (2 * cells), i] += factor
            derive[(i - offset) % (2 * cells), i] -= factor
    return (
        np.concatenate([refine, refine @ derive], axis=1).astype(np.float32),
        derive.astype(np.float32),
    )


def density_kernel(scale, which_ref, occupations_ref, orbitals_ref, out_ref):
    total = None
    for band in range(orbitals_ref.shape[0]):
        value = orbitals_ref[band, :, 0].astype(jnp.float32)
        term = (occupations_ref[band] * scale) * (value * value)
        total = term if total is None else total + term
    out_ref[...] = total


def partial_density(orbitals, occupations, which, scale):
    bands, blocks, _, rows, columns, lanes = orbitals.shape
    group = 2 if blocks % 2 == 0 else 1
    return pl.pallas_call(
        functools.partial(density_kernel, scale),
        out_shape=jax.ShapeDtypeStruct((blocks, rows, columns, lanes), jnp.float32),
        grid_spec=pltpu.PrefetchScalarGridSpec(
            num_scalar_prefetch=1,
            grid=(blocks // group,),
            in_specs=[
                pl.BlockSpec(memory_space=pltpu.SMEM),
                pl.BlockSpec(
                    (bands, group, 1, rows, columns, lanes),
                    lambda g, which_ref: (0, g, which_ref[0], 0, 0, 0),
                ),
            ],
            out_specs=pl.BlockSpec((group, rows, columns, lanes), lambda g, which_ref: (g, 0, 0, 0)),
        ),
        cost_estimate=pl.CostEstimate(
            flops=4 * bands * blocks * rows * columns * lanes,
            bytes_accessed=(2 * bands + 4) * blocks * rows * columns * lanes,
            transcendentals=0,
        ),
    )(which, occupations, orbitals)


def difference(load):
    total = None
    for offset, factor in zip((1, 2, 3, 4), deriv_factors):
        term = factor * (load(offset) - load(-offset))
        total = term if total is None else total + term
    return total


def stencil(load):
    a = load(0) + load(1)
    b = load(-1) + load(2)
    c = load(-2) + load(3)
    return interp_weights[2] * a + interp_weights[1] * b + interp_weights[0] * c


def tail_kernel(counts, *refs):
    pieces = refs[: len(counts)]
    refine_ref, derive_ref, out_ref, rows_ref, mixed_ref, fine_ref, grad_ref, flux_ref, side_ref, third_ref, local_ref = refs[len(counts) :]
    layers = [(piece, row) for piece, count in zip(pieces, counts) for row in range(count)]
    extent_a, extent_b, _ = out_ref.shape
    lanes = pieces[0].shape[2]
    wide_a, wide_b = extent_a + 16, extent_b + 16
    half_b = wide_b // 2

    def coarse(index):
        piece, row = layers[index]
        return piece[row]

    for index in range(wide_a):
        at = index // 2 + 2
        if index % 2 == 0:
            rows_ref[index] = coarse(at)
        else:
            rows_ref[index] = stencil(lambda offset: coarse(at + offset))
        first = SIDE - 4
        mixed_ref[index, pl.ds(0, half_b, stride=2), :] = rows_ref[index, first : first + half_b, :]
        mixed_ref[index, pl.ds(1, half_b, stride=2), :] = stencil(
            lambda offset: rows_ref[index, first + offset : first + offset + half_b, :]
        )
    for index in range(wide_a):
        inner = 4 <= index < wide_a - 4
        matrix = refine_ref[...] if inner else refine_ref[:, : 2 * lanes]
        product = jnp.dot(mixed_ref[index], matrix, preferred_element_type=jnp.float32, precision=HIGHEST)
        for half in range(2):
            fine_ref[half, index] = product[:, half * lanes : (half + 1) * lanes]
            if inner:
                grad_ref[half, index - 4] = product[:, (2 + half) * lanes : (3 + half) * lanes]
    for index in range(extent_a + 8):
        own = 4 <= index < extent_a + 4
        low, high = (4, wide_b - 4) if own else (8, wide_b - 8)
        for half in range(2):
            at = index + 4
            density = fine_ref[half, at, low:high, :]
            grad_a = difference(lambda offset: fine_ref[half, at + offset, low:high, :])
            grad_b = difference(lambda offset: fine_ref[half, at, low + offset : high + offset, :])
            grad_c = grad_ref[half, index, low:high, :]
            shifted = density * density + 0.01
            root = jnp.exp(jnp.log(shifted) * (1.0 / 6.0))
            scaling = 0.01 * (shifted * (root * root))
            square = grad_a * grad_a + grad_b * grad_b + grad_c * grad_c
            inverse = 1.0 / (scaling + (0.2195 / 0.804) * square)
            ratio = scaling * inverse
            weight = 0.2195 * (ratio * inverse)
            flux_ref[half, index, low:high, :] = weight * grad_a
            if own:
                side_ref[half, index - 4, low:high, :] = weight * grad_b
                third_ref[half, index - 4, low:high, :] = weight * grad_c
                local_ref[half, index - 4, low:high, :] = -0.75 * root * (1.804 - 0.804 * ratio)
    for index in range(extent_a):
        third = jnp.concatenate([third_ref[half, index, 8 : 8 + extent_b, :] for half in range(2)], axis=1)
        third = jnp.dot(third, derive_ref[...], preferred_element_type=jnp.float32, precision=HIGHEST)
        for half in range(2):
            part = slice(half * lanes, (half + 1) * lanes)
            total = difference(lambda offset: flux_ref[half, index + 4 + offset, 8 : 8 + extent_b, :])
            total = total + difference(lambda offset: side_ref[half, index, 8 + offset : 8 + offset + extent_b, :])
            out_ref[index, :, part] = local_ref[half, index, 8 : 8 + extent_b, :] + 0.2 * (total + third[:, part])


def tail(pieces, counts, rows, columns):
    lanes = pieces[0].shape[2]
    extent_a, extent_b = 2 * rows, 2 * columns
    wide_a, wide_b = extent_a + 16, extent_b + 16
    refine, derive = third_matrices(lanes)
    points = wide_a * wide_b * 2 * lanes
    scratch = lambda *shape: pltpu.VMEM(shape, jnp.float32)
    return pl.pallas_call(
        functools.partial(tail_kernel, counts),
        out_shape=jax.ShapeDtypeStruct((extent_a, extent_b, 2 * lanes), jnp.float32),
        in_specs=[pl.BlockSpec(memory_space=pltpu.VMEM)] * (len(pieces) + 2),
        out_specs=pl.BlockSpec(memory_space=pltpu.VMEM),
        scratch_shapes=[
            scratch(wide_a, columns + 2 * SIDE, lanes),
            scratch(wide_a, wide_b, lanes),
            scratch(2, wide_a, wide_b, lanes),
            scratch(2, extent_a + 8, wide_b, lanes),
            scratch(2, extent_a + 8, wide_b, lanes),
            scratch(2, extent_a, wide_b, lanes),
            scratch(2, extent_a, wide_b, lanes),
            scratch(2, extent_a, wide_b, lanes),
        ],
        cost_estimate=pl.CostEstimate(
            flops=100 * points, bytes_accessed=8 * points, transcendentals=2 * points
        ),
    )(*pieces, jnp.asarray(refine), jnp.asarray(derive))


def shift(value, axis, step):
    devices = lax.axis_size(axis)
    return lax.ppermute(value, axis, [(i, (i + step) % devices) for i in range(devices)])


def with_sides(block):
    columns, devices = block.shape[1], lax.axis_size("dom")
    last, first = block[:, columns - SIDE :], block[:, :SIDE]
    if devices == 1:
        before, after = last, first
    elif devices == 2:
        other = shift(block, "dom", 1)
        before, after = other[:, columns - SIDE :], other[:, :SIDE]
    else:
        before, after = shift(last, "dom", 1), shift(first, "dom", -1)
    return jnp.concatenate([before, block, after], axis=1)


def with_layers(block):
    rows = block.shape[0]
    before, after = [], []
    step, missing = 1, BEFORE
    while missing > 0:
        count = min(rows, missing)
        before.insert(0, shift(block[rows - count :], "band", step))
        step, missing = step + 1, missing - count
    step, missing = 1, AFTER
    while missing > 0:
        count = min(rows, missing)
        after.append(shift(block[:count], "band", -step))
        step, missing = step + 1, missing - count
    return before + [block] + after


def on_device(orbitals, occupations):
    devices = lax.axis_size("band")
    bands, layers, columns, lanes = orbitals.shape
    rows = layers // devices
    place = lax.axis_index("band")
    scale = 1.0 / (bands * devices)
    blocks = orbitals.reshape(bands, devices // 2, 2, rows, columns, lanes)
    parity = lax.rem(place, 2)
    send = partial_density(blocks, occupations, jnp.reshape(1 - parity, (1,)).astype(jnp.int32), scale)
    keep = partial_density(blocks, occupations, jnp.reshape(parity, (1,)).astype(jnp.int32), scale)
    width = 1
    while True:
        density = keep + lax.ppermute(send, "band", [(i, i ^ width) for i in range(devices)])
        width = 2 * width
        if width == devices:
            break
        bit = lax.rem(lax.div(place, width), 2)
        pairs = density.reshape((devices // width // 2, 2, rows, columns, lanes))
        keep = lax.dynamic_index_in_dim(pairs, bit, 1, False)
        send = lax.dynamic_index_in_dim(pairs, 1 - bit, 1, False)
    block = with_sides(density[0])
    pieces = with_layers(block)
    return tail(pieces, tuple(piece.shape[0] for piece in pieces), rows, columns)


def solution(mesh):
    return jax.shard_map(
        on_device,
        mesh=mesh,
        in_specs=(P("band", None, "dom", None), P("band")),
        out_specs=P("band", "dom", None),
        check_vma=False,
    )
```

time: 119 us -> 49.2 us (0.41)
  waiting for transfers between devices: 78.5 us -> 17.3 us
  between operations: 13.6 us -> 0.09 us
  Pallas kernels: 0 us -> 12.7 us
  other arithmetic: 10.6 us -> 1.03 us
  starting transfers between devices: 10.9 us -> 16.4 us
  local copies, waits for them, and re-layouts: 5.29 us -> 1.31 us
    reduce_scatter x1 -> x0, waiting for transfers between devices: 59.5 us -> none  [on_device(): lax.psum_scatter(jnp.sum(weights[:, None, None, None] * jnp.square(orbita...]
    pallas_call x0 -> x3, Pallas kernels: none -> 12.7 us  [the longest x2 6.67 us: partial_density(): pl.pallas_call(functools.partial(density_kernel, scale), out_shape=jax.Sh...]
    ppermute x8 -> x9, starting transfers between devices: 10.9 us -> 16.4 us  [the longest x5 8.58 us: shift(): lax.ppermute(value, axis, [(i, (i + step) % devices) for i in range(devic...]
    mul x2 -> x0, other arithmetic: 4.6 us -> none  [the longest x1 3.71 us: pointwise(): flux_weight * grad_c]
    slice x19 -> x3, local copies, waits for them, and re-layouts: 3.48 us -> 0.01 us  [the longest x1 0.01 us: with_layers(): after.append(shift(block[:count], 'band', -step))]
    reduce_sum x1 -> x0, other arithmetic: 3.02 us -> none  [on_device(): jnp.sum(weights[:, None, None, None] * jnp.square(orbitals.astype(jnp.flo...]
    ppermute x8 -> x9, waiting for transfers between devices: 19 us -> 17.3 us  [the longest x5 8.76 us: shift(): lax.ppermute(value, axis, [(i, (i + step) % devices) for i in range(devic...]
  transfers between devices with their start and end apart: 9 -> 9, of which waited for: 8 -> 5; matrix products, arithmetic and copies ran while one was open for 1% -> 0% of each run, Pallas kernels for 0% -> 7%
where the time goes in v1:
time: 49.2 us; the launch traced here: 48.9 us
  waiting for transfers between devices  17.3 us (35%)
  starting transfers between devices  16.4 us (33%)
  Pallas kernels  12.7 us (26%)
  local copies, waits for them, and re-layouts  1.31 us (3%)
  other arithmetic  1.03 us (2%)
    ppermute x5, waiting for transfers between devices, shift(): lax.ppermute(value, axis, [(i, (i + step) % devices) for i in range(devic...  8.76 us
    ppermute x5, starting transfers between devices, shift(): lax.ppermute(value, axis, [(i, (i + step) % devices) for i in range(devic...  8.58 us
    ppermute x4, waiting for transfers between devices, on_device(): lax.ppermute(send, 'band', [(i, i ^ width) for i in range(devices)])  8.57 us
    ppermute x4, starting transfers between devices, on_device(): lax.ppermute(send, 'band', [(i, i ^ width) for i in range(devices)])  7.85 us
    pallas_call x2, Pallas kernels, partial_density(): pl.pallas_call(functools.partial(density_kernel, scale), out_shape=jax.Sh...  6.67 us
    pallas_call x1, Pallas kernels, tail(): pl.pallas_call(functools.partial(tail_kernel, counts), out_shape=jax.Shap...  6.05 us
    unnamed x10, local copies, waits for them, and re-layouts  1.25 us
    add x3, other arithmetic, on_device(): keep + lax.ppermute(send, 'band', [(i, i ^ width) for i in range(devices)])  1.01 us
  transfers between devices with their start and end apart: 9, of which 5 were waited for; matrix products, arithmetic and copies ran while one was open for 0% of the time, Pallas kernels for 7%

profile of v1, /device:TPU:0, one launch (start us, length us, event | category | flops | bytes accessed | tf_op | source)
XLA Modules:
  0.0 48.9 jit_solution(9605628091851262302)
XLA Ops:
  0.0 3.3 %shard_map.47 = f32[8,4,16,128]{3,2,1,0:T(8,128)} custom-call(s32[1]{0:T(128)} %bitcast.2.which_ref, f32[8]{0:T(128)} %occupations_ref.3, bf16[8,8,2,4,16,128]{5,4,3,2,1,0:T(8,128)(2,1)} %bitcast.15), custom_call_target="tpu_custom_call" | custom-call | flops 2097152 | bytes 1310720 | tf_op jit(solution)/shard_map/pallas_call | solution.py:54
  3.3 0.5 %collective-permute-start = (f32[8,4,16,128]{3,2,1,0:T(8,128)}, f32[8,4,16,128]{3,2,1,0:T(8,128)S(1)}, u32[]{:S(2)}, u32[]{:S(2)}) collective-permute-start(f32[8,4,16,128]{3,2,1,0:T(8,128)} %shard_map.47), channel_id=1, source_target_pairs={{0,2},{2,0},{4,6},{6,4},{8,10},{10,8},{12,14},{14,12},{16,18},{18,... | collective-permute-start | bytes 786440 | tf_op jit(solution)/shard_map/ppermute | solution.py:229
  3.8 3.3 %shard_map.46 = f32[8,4,16,128]{3,2,1,0:T(8,128)} custom-call(s32[1]{0:T(128)} %bitcast.which_ref, f32[8]{0:T(128)} %occupations_ref.3, bf16[8,8,2,4,16,128]{5,4,3,2,1,0:T(8,128)(2,1)} %bitcast.16), custom_call_target="tpu_custom_call" | custom-call | flops 2097152 | bytes 1310720 | tf_op jit(solution)/shard_map/pallas_call | solution.py:54
  7.2 1.0 %add.36 = f32[8,4,16,128]{3,2,1,0:T(8,128)S(1)} add(f32[8,4,16,128]{3,2,1,0:T(8,128)} %shard_map.46, f32[8,4,16,128]{3,2,1,0:T(8,128)S(1)} %collective-permute-done) | non-fusion elementwise | flops 65536 | bytes 786432 | tf_op jit(solution)/shard_map/add | solution.py:229
  8.2 2.6 %collective-permute-start.1 = (f32[4,4,16,128]{3,2,1,0:T(8,128)S(1)}, f32[4,4,16,128]{3,2,1,0:T(8,128)S(1)}, u32[]{:S(2)}, u32[]{:S(2)}) collective-permute-start(f32[4,4,16,128]{3,2,1,0:T(8,128)S(1)} %dynamic-slice_bitcast_fusion), channel_id=1, source_target_pairs={{0,4},{2,6},{4,0},{6,2},{8,12},{10,14},{12,8},{14,10},{16,20},{18,... | collective-permute-start | bytes 393224 | tf_op jit(solution)/shard_map/ppermute | solution.py:229
  10.7 4.2 %collective-permute-done.1 = f32[4,4,16,128]{3,2,1,0:T(8,128)S(1)} collective-permute-done((f32[4,4,16,128]{3,2,1,0:T(8,128)S(1)}, f32[4,4,16,128]{3,2,1,0:T(8,128)S(1)}, u32[]{:S(2)}, u32[]{:S(2)}) %collective-permute-start.1) | collective-permute-done | bytes 131104 | tf_op jit(solution)/shard_map/ppermute | solution.py:229
  14.9 1.9 %collective-permute-start.2 = (f32[2,4,16,128]{3,2,1,0:T(8,128)S(1)}, f32[2,4,16,128]{3,2,1,0:T(8,128)S(1)}, u32[]{:S(2)}, u32[]{:S(2)}) collective-permute-start(f32[2,4,16,128]{3,2,1,0:T(8,128)S(1)} %dynamic-slice_bitcast_fusion.1), channel_id=1, source_target_pairs={{0,8},{2,10},{4,12},{6,14},{8,0},{10,2},{12,4},{14,6},{16,24},{18,... | collective-permute-start | bytes 196616 | tf_op jit(solution)/shard_map/ppermute | solution.py:229
  16.8 2.4 %collective-permute-done.2 = f32[2,4,16,128]{3,2,1,0:T(8,128)S(1)} collective-permute-done((f32[2,4,16,128]{3,2,1,0:T(8,128)S(1)}, f32[2,4,16,128]{3,2,1,0:T(8,128)S(1)}, u32[]{:S(2)}, u32[]{:S(2)}) %collective-permute-start.2) | collective-permute-done | bytes 65568 | tf_op jit(solution)/shard_map/ppermute | solution.py:229
  19.3 2.9 %collective-permute-start.3 = (f32[1,4,16,128]{3,2,1,0:T(8,128)S(1)}, f32[1,4,16,128]{3,2,1,0:T(8,128)S(1)}, u32[]{:S(2)}, u32[]{:S(2)}) collective-permute-start(f32[1,4,16,128]{3,2,1,0:T(8,128)S(1)} %constant_dynamic-slice_fusion), channel_id=1, source_target_pairs={{0,16},{2,18},{4,20},{6,22},{8,24},{10,26},{12,28},{14,30},{16,0},... | collective-permute-start | bytes 98312 | tf_op jit(solution)/shard_map/ppermute | solution.py:229
  22.2 2.0 %collective-permute-done.3 = f32[1,4,16,128]{3,2,1,0:T(8,128)S(1)} collective-permute-done((f32[1,4,16,128]{3,2,1,0:T(8,128)S(1)}, f32[1,4,16,128]{3,2,1,0:T(8,128)S(1)}, u32[]{:S(2)}, u32[]{:S(2)}) %collective-permute-start.3) | collective-permute-done | bytes 32800 | tf_op jit(solution)/shard_map/ppermute | solution.py:229
  24.2 1.8 %collective-permute-start.4 = (f32[4,16,128]{2,1,0:T(8,128)S(1)}, f32[4,16,128]{2,1,0:T(8,128)S(1)}, u32[]{:S(2)}, u32[]{:S(2)}) collective-permute-start(f32[4,16,128]{2,1,0:T(8,128)S(1)} %add_bitcast_fusion), channel_id=1, source_target_pairs={{0,1},{1,0},{2,3},{3,2},{4,5},{5,4},{6,7},{7,6},{8,9},{9,8},{10,11... | collective-permute-start | bytes 98312 | tf_op jit(solution)/shard_map/ppermute | solution.py:185
  26.0 2.1 %collective-permute-done.4 = f32[4,16,128]{2,1,0:T(8,128)S(1)} collective-permute-done((f32[4,16,128]{2,1,0:T(8,128)S(1)}, f32[4,16,128]{2,1,0:T(8,128)S(1)}, u32[]{:S(2)}, u32[]{:S(2)}) %collective-permute-start.4) | collective-permute-done | bytes 32800 | tf_op jit(solution)/shard_map/ppermute | solution.py:185
  28.1 0.1 collective-permute-start.6
  28.2 4.4 %collective-permute-start.7 = (f32[4,32,128]{2,1,0:T(8,128)S(1)}, f32[4,32,128]{2,1,0:T(8,128)S(1)}, u32[]{:S(2)}, u32[]{:S(2)}) collective-permute-start(f32[4,32,128]{2,1,0:T(8,128)S(1)} %pad_maximum_fusion.refs_2_), channel_id=1, source_target_pairs={{0,30},{2,0},{4,2},{6,4},{8,6},{10,8},{12,10},{14,12},{16,14},{18,... | collective-permute-start | bytes 196616 | tf_op jit(solution)/shard_map/ppermute | solution.py:185
  32.6 2.3 %collective-permute-start.8 = (f32[3,32,128]{2,1,0:T(8,128)S(1)}, f32[3,32,128]{2,1,0:T(8,128)S(1)}, u32[]{:S(2)}, u32[]{:S(2)}) collective-permute-start(f32[3,32,128]{2,1,0:T(8,128)S(1)} %slice.19), channel_id=1, source_target_pairs={{0,28},{2,30},{4,0},{6,2},{8,4},{10,6},{12,8},{14,10},{16,12},{18,... | collective-permute-start | bytes 147464 | tf_op jit(solution)/shard_map/ppermute | solution.py:185
  35.0 0.0 collective-permute-start.5
  35.0 6.6 %collective-permute-done.5.refs_0_ = f32[2,32,128]{2,1,0:T(8,128)S(1)} collective-permute-done((f32[2,32,128]{2,1,0:T(8,128)S(1)}, f32[2,32,128]{2,1,0:T(8,128)S(1)}, u32[]{:S(2)}, u32[]{:S(2)}) %collective-permute-start.5) | collective-permute-done | bytes 32800 | tf_op jit(solution)/shard_map/ppermute | solution.py:185
  41.6 0.0 collective-permute-done.8.refs_4_
  41.6 0.0 collective-permute-done.6.refs_1_
  41.6 0.6 %copy-done.4 = f32[2,32,128]{2,1,0:T(8,128)} copy-done((f32[2,32,128]{2,1,0:T(8,128)}, f32[2,32,128]{2,1,0:T(8,128)S(1)}, u32[]{:S(2)}) %copy-start.4) | copy-done | bytes 32792
  42.2 0.0 copy-done.3
  42.2 0.0 copy-done.1
  42.2 0.6 %copy-done.2 = f32[4,32,128]{2,1,0:T(8,128)} copy-done((f32[4,32,128]{2,1,0:T(8,128)}, f32[4,32,128]{2,1,0:T(8,128)S(1)}, u32[]{:S(2)}) %copy-start.2) | copy-done | bytes 65560
  42.9 6.1 %shard_map.48 = f32[8,32,256]{2,1,0:T(8,128)} custom-call(f32[2,32,128]{2,1,0:T(8,128)} %copy-done.4, f32[4,32,128]{2,1,0:T(8,128)} %copy-done.1, f32[4,32,128]{2,1,0:T(8,128)} %copy-done, f32[4,32,128]{2,1,0:T(8,128)} %copy-done.2, f32[3,32,128]{2,1,0:T(8,128)} %copy-done.3, f32[128,512]{1,0:T(8,128)} %constant.53.clone.refs_5_, ...), custom_call_target="tpu_custom_call" | custom-call | flops 29491200 | bytes 2359296 | tf_op jit(solution)/shard_map/pallas_call | solution.py:162
  (18 shorter events, 0.1 us)
Async XLA Ops:
  3.3 3.8 %collective-permute-start = (f32[8,4,16,128]{3,2,1,0:T(8,128)}, f32[8,4,16,128]{3,2,1,0:T(8,128)S(1)}, u32[]{:S(2)}, u32[]{:S(2)}) collective-permute-start(f32[8,4,16,128]{3,2,1,0:T(8,128)} %shard_map.47), channel_id=1, source_target_pairs={{0,2},{2,0},{4,6},{6,4},{8,10},{10,8},{12,14},{14,12},{16,18},{18,... | collective-permute-start | bytes 786440 | tf_op jit(solution)/shard_map/ppermute | solution.py:229
  8.2 6.7 %collective-permute-start.1 = (f32[4,4,16,128]{3,2,1,0:T(8,128)S(1)}, f32[4,4,16,128]{3,2,1,0:T(8,128)S(1)}, u32[]{:S(2)}, u32[]{:S(2)}) collective-permute-start(f32[4,4,16,128]{3,2,1,0:T(8,128)S(1)} %dynamic-slice_bitcast_fusion), channel_id=1, source_target_pairs={{0,4},{2,6},{4,0},{6,2},{8,12},{10,14},{12,8},{14,10},{16,20},{18,... | collective-permute-start | bytes 393224 | tf_op jit(solution)/shard_map/ppermute | solution.py:229
  14.9 4.3 %collective-permute-start.2 = (f32[2,4,16,128]{3,2,1,0:T(8,128)S(1)}, f32[2,4,16,128]{3,2,1,0:T(8,128)S(1)}, u32[]{:S(2)}, u32[]{:S(2)}) collective-permute-start(f32[2,4,16,128]{3,2,1,0:T(8,128)S(1)} %dynamic-slice_bitcast_fusion.1), channel_id=1, source_target_pairs={{0,8},{2,10},{4,12},{6,14},{8,0},{10,2},{12,4},{14,6},{16,24},{18,... | collective-permute-start | bytes 196616 | tf_op jit(solution)/shard_map/ppermute | solution.py:229
  19.3 4.9 %collective-permute-start.3 = (f32[1,4,16,128]{3,2,1,0:T(8,128)S(1)}, f32[1,4,16,128]{3,2,1,0:T(8,128)S(1)}, u32[]{:S(2)}, u32[]{:S(2)}) collective-permute-start(f32[1,4,16,128]{3,2,1,0:T(8,128)S(1)} %constant_dynamic-slice_fusion), channel_id=1, source_target_pairs={{0,16},{2,18},{4,20},{6,22},{8,24},{10,26},{12,28},{14,30},{16,0},... | collective-permute-start | bytes 98312 | tf_op jit(solution)/shard_map/ppermute | solution.py:229
  24.2 3.9 %collective-permute-start.4 = (f32[4,16,128]{2,1,0:T(8,128)S(1)}, f32[4,16,128]{2,1,0:T(8,128)S(1)}, u32[]{:S(2)}, u32[]{:S(2)}) collective-permute-start(f32[4,16,128]{2,1,0:T(8,128)S(1)} %add_bitcast_fusion), channel_id=1, source_target_pairs={{0,1},{1,0},{2,3},{3,2},{4,5},{5,4},{6,7},{7,6},{8,9},{9,8},{10,11... | collective-permute-start | bytes 98312 | tf_op jit(solution)/shard_map/ppermute | solution.py:185
  28.1 13.5 %copy-start = (f32[4,32,128]{2,1,0:T(8,128)}, f32[4,32,128]{2,1,0:T(8,128)S(1)}, u32[]{:S(2)}) copy-start(f32[4,32,128]{2,1,0:T(8,128)S(1)} %pad_maximum_fusion.refs_2_) | copy-start | bytes 196612
  28.1 13.4 %collective-permute-start.6 = (f32[4,32,128]{2,1,0:T(8,128)S(1)}, f32[4,32,128]{2,1,0:T(8,128)S(1)}, u32[]{:S(2)}, u32[]{:S(2)}) collective-permute-start(f32[4,32,128]{2,1,0:T(8,128)S(1)} %pad_maximum_fusion.refs_2_), channel_id=1, source_target_pairs={{0,2},{2,4},{4,6},{6,8},{8,10},{10,12},{12,14},{14,16},{16,18},{18... | collective-permute-start | bytes 196616 | tf_op jit(solution)/shard_map/ppermute | solution.py:185
  28.2 13.4 %collective-permute-start.7 = (f32[4,32,128]{2,1,0:T(8,128)S(1)}, f32[4,32,128]{2,1,0:T(8,128)S(1)}, u32[]{:S(2)}, u32[]{:S(2)}) collective-permute-start(f32[4,32,128]{2,1,0:T(8,128)S(1)} %pad_maximum_fusion.refs_2_), channel_id=1, source_target_pairs={{0,30},{2,0},{4,2},{6,4},{8,6},{10,8},{12,10},{14,12},{16,14},{18,... | collective-permute-start | bytes 196616 | tf_op jit(solution)/shard_map/ppermute | solution.py:185
  32.6 8.9 %collective-permute-start.8 = (f32[3,32,128]{2,1,0:T(8,128)S(1)}, f32[3,32,128]{2,1,0:T(8,128)S(1)}, u32[]{:S(2)}, u32[]{:S(2)}) collective-permute-start(f32[3,32,128]{2,1,0:T(8,128)S(1)} %slice.19), channel_id=1, source_target_pairs={{0,28},{2,30},{4,0},{6,2},{8,4},{10,6},{12,8},{14,10},{16,12},{18,... | collective-permute-start | bytes 147464 | tf_op jit(solution)/shard_map/ppermute | solution.py:185
  35.0 6.6 %collective-permute-start.5 = (f32[2,32,128]{2,1,0:T(8,128)S(1)}, f32[2,32,128]{2,1,0:T(8,128)S(1)}, u32[]{:S(2)}, u32[]{:S(2)}) collective-permute-start(f32[2,32,128]{2,1,0:T(8,128)S(1)} %slice.18), channel_id=1, source_target_pairs={{0,4},{2,6},{4,8},{6,10},{8,12},{10,14},{12,16},{14,18},{16,20},{1... | collective-permute-start | bytes 98312 | tf_op jit(solution)/shard_map/ppermute | solution.py:185
  41.6 0.6 %copy-start.4 = (f32[2,32,128]{2,1,0:T(8,128)}, f32[2,32,128]{2,1,0:T(8,128)S(1)}, u32[]{:S(2)}) copy-start(f32[2,32,128]{2,1,0:T(8,128)S(1)} %collective-permute-done.5.refs_0_) | copy-start | bytes 98308
  41.6 0.6 %copy-start.3 = (f32[3,32,128]{2,1,0:T(8,128)}, f32[3,32,128]{2,1,0:T(8,128)S(1)}, u32[]{:S(2)}) copy-start(f32[3,32,128]{2,1,0:T(8,128)S(1)} %collective-permute-done.8.refs_4_) | copy-start | bytes 147460
  41.6 0.7 %copy-start.1 = (f32[4,32,128]{2,1,0:T(8,128)}, f32[4,32,128]{2,1,0:T(8,128)S(1)}, u32[]{:S(2)}) copy-start(f32[4,32,128]{2,1,0:T(8,128)S(1)} %collective-permute-done.6.refs_1_) | copy-start | bytes 196612
  42.2 0.6 %copy-start.2 = (f32[4,32,128]{2,1,0:T(8,128)}, f32[4,32,128]{2,1,0:T(8,128)S(1)}, u32[]{:S(2)}) copy-start(f32[4,32,128]{2,1,0:T(8,128)S(1)} %collective-permute-done.7.refs_3_) | copy-start | bytes 196612

commit v2 on v1

v2 whole, which is shorter than its diff:
```python
import functools

import jax
import jax.numpy as jnp
import ml_dtypes
import numpy as np
from jax import lax
from jax.experimental import pallas as pl
from jax.experimental.pallas import tpu as pltpu
from jax.sharding import PartitionSpec as P

interp_weights = (
    3.0 / 256.0,
    -25.0 / 256.0,
    150.0 / 256.0,
    150.0 / 256.0,
    -25.0 / 256.0,
    3.0 / 256.0,
)
deriv_factors = (4.0 / 5.0, -1.0 / 5.0, 4.0 / 105.0, -1.0 / 280.0)
BEFORE, AFTER = 6, 7
VMEM_LIMIT = 16 * 1024 * 1024
bf16 = ml_dtypes.bfloat16


def split_matrix(matrix):
    high = matrix.astype(bf16)
    return high, (matrix - high.astype(np.float64)).astype(bf16)


def third_matrices(cells):
    refine = np.zeros((cells, 2 * cells))
    for i in range(cells):
        refine[i, 2 * i] = 1.0
        for offset, factor in zip(range(-2, 4), interp_weights):
            refine[(i + offset) % cells, 2 * i + 1] += factor
    derive = np.zeros((2 * cells, 2 * cells))
    for i in range(2 * cells):
        for offset, factor in zip((1, 2, 3, 4), deriv_factors):
            derive[(i + offset) % (2 * cells), i] += factor
            derive[(i - offset) % (2 * cells), i] -= factor
    twice = lambda matrix: np.concatenate([matrix, matrix], axis=0)
    both = split_matrix(twice(refine @ derive))
    return np.concatenate([twice(refine).astype(bf16), *both, *split_matrix(derive)], axis=1)


def density_kernel(scale, other, occupations_ref, orbitals_ref, out_ref, buffer_ref, sems):
    bands, layers, half, _ = buffer_ref.shape
    core = lax.rem(lax.axis_index("band"), 2)
    start = pl.multiple_of((1 - core if other else core) * half, half)
    chunk = layers // sems.shape[0]
    copies = []
    for index in range(sems.shape[0]):
        rows = pl.ds(index * chunk, chunk)
        copy = pltpu.make_async_copy(
            orbitals_ref.at[:, rows, pl.ds(start, half), :], buffer_ref.at[:, rows], sems.at[index]
        )
        copy.start()
        copies.append(copy)
    for index, copy in enumerate(copies):
        copy.wait()
        rows = slice(index * chunk, (index + 1) * chunk)
        total = None
        for band in range(bands):
            value = buffer_ref[band, rows].astype(jnp.float32)
            term = (occupations_ref[band] * scale) * (value * value)
            total = term if total is None else total + term
        out_ref[rows] = total


def partial_density(orbitals, occupations, scale, other):
    bands, layers, columns, lanes = orbitals.shape
    half = columns // 2
    points = layers * half * lanes
    return pl.pallas_call(
        functools.partial(density_kernel, scale, other),
        out_shape=jax.ShapeDtypeStruct((layers, half, lanes), jnp.float32),
        in_specs=[pl.BlockSpec(memory_space=pltpu.SMEM), pl.BlockSpec(memory_space=pl.ANY)],
        out_specs=pl.BlockSpec(memory_space=pltpu.VMEM),
        scratch_shapes=[pltpu.VMEM((bands, layers, half, lanes), orbitals.dtype), pltpu.SemaphoreType.DMA((4,))],
        compiler_params=pltpu.CompilerParams(vmem_limit_bytes=VMEM_LIMIT),
        cost_estimate=pl.CostEstimate(
            flops=4 * bands * points, bytes_accessed=(2 * bands + 4) * points, transcendentals=0
        ),
    )(occupations, orbitals)


def combine_kernel(planes, keep_ref, other_ref, *out_refs):
    layers, count = keep_ref.shape[0], out_refs[0].shape[0]
    plane = lax.div(lax.axis_index("band"), 4)
    for step, out_ref in enumerate(out_refs):
        first = lax.rem(plane + step, planes) * (layers // planes) + (layers - BEFORE)
        for row in range(count):
            at = lax.rem(first + row, layers)
            out_ref[row] = keep_ref[at] + other_ref[at]


def combine(keep, other, planes):
    layers, half, lanes = keep.shape
    shape = jax.ShapeDtypeStruct((layers // planes + BEFORE + AFTER, half, lanes), jnp.float32)
    return pl.pallas_call(
        functools.partial(combine_kernel, planes),
        out_shape=[shape] * planes,
        in_specs=[pl.BlockSpec(memory_space=pltpu.VMEM)] * 2,
        out_specs=[pl.BlockSpec(memory_space=pltpu.VMEM)] * planes,
        compiler_params=pltpu.CompilerParams(vmem_limit_bytes=VMEM_LIMIT),
    )(keep, other)


def difference(load):
    total = None
    for offset, factor in zip((1, 2, 3, 4), deriv_factors):
        term = factor * (load(offset) - load(-offset))
        total = term if total is None else total + term
    return total


def stencil(load):
    a = load(0) + load(1)
    b = load(-1) + load(2)
    c = load(-2) + load(3)
    return interp_weights[2] * a + interp_weights[1] * b + interp_weights[0] * c


def split_value(value):
    high = value.astype(jnp.bfloat16)
    return high, (value - high.astype(jnp.float32)).astype(jnp.bfloat16)


def product(left, right):
    return jnp.dot(left, right, preferred_element_type=jnp.float32)


def tail_kernel(mine_ref, other_ref, matrix_ref, out_ref, coarse_ref, rows_ref, mixed_ref, fine_ref, grad_ref, flux_ref, side_ref, third_ref, local_ref):
    extent_a, extent_b, _ = out_ref.shape
    half, lanes = mine_ref.shape[2:]
    wide_a, wide_b = extent_a + 16, extent_b + 16
    half_b = wide_b // 2
    core = lax.rem(lax.axis_index("band"), 2)
    for tile, (owner, side) in enumerate(((1, 1), (0, 0), (1, 0), (0, 1))):
        coarse_ref[:, tile * half : (tile + 1) * half, :] = jnp.where(
            core == owner, mine_ref[side], other_ref[side]
        )
    first = half - 4
    for index in range(wide_a):
        at = index // 2 + BEFORE - 4
        if index % 2 == 0:
            rows_ref[index] = coarse_ref[at]
        else:
            rows_ref[index] = stencil(lambda offset: coarse_ref[at + offset])
        mixed_ref[index, pl.ds(0, half_b, stride=2), :] = rows_ref[index, first : first + half_b, :]
        mixed_ref[index, pl.ds(1, half_b, stride=2), :] = stencil(
            lambda offset: rows_ref[index, first + offset : first + offset + half_b, :]
        )
    wide = 2 * lanes
    group = 4
    for start in range(0, wide_a, group):
        value = mixed_ref[start : start + group].reshape(group * wide_b, lanes)
        value = jnp.concatenate(split_value(value), axis=1)
        fine = product(value, matrix_ref[:, :wide]).reshape(group, wide_b, wide)
        for part in range(2):
            fine_ref[part, start : start + group] = fine[:, :, part * lanes : (part + 1) * lanes]
        if 4 <= start < wide_a - 4:
            grad = product(value, matrix_ref[:, wide : 2 * wide]) + product(value, matrix_ref[:, 2 * wide : 3 * wide])
            grad = grad.reshape(group, wide_b, wide)
            for part in range(2):
                grad_ref[part, start - 4 : start - 4 + group] = grad[:, :, part * lanes : (part + 1) * lanes]
    for index in range(extent_a + 8):
        own = 4 <= index < extent_a + 4
        low, high = (4, wide_b - 4) if own else (8, wide_b - 8)
        for part in range(2):
            at = index + 4
            density = fine_ref[part, at, low:high, :]
            grad_a = difference(lambda offset: fine_ref[part, at + offset, low:high, :])
            grad_b = difference(lambda offset: fine_ref[part, at, low + offset : high + offset, :])
            grad_c = grad_ref[part, index, low:high, :]
            shifted = density * density + 0.01
            root = jnp.exp(jnp.log(shifted) * (1.0 / 6.0))
            scaling = 0.01 * (shifted * (root * root))
            square = grad_a * grad_a + grad_b * grad_b + grad_c * grad_c
            inverse = 1.0 / (scaling + (0.2195 / 0.804) * square)
            ratio = scaling * inverse
            weight = 0.2195 * (ratio * inverse)
            flux_ref[part, index, low:high, :] = weight * grad_a
            if own:
                side_ref[part, index - 4, low:high, :] = weight * grad_b
                third_ref[part, index - 4, low:high, :] = weight * grad_c
                local_ref[part, index - 4, low:high, :] = -0.75 * root * (1.804 - 0.804 * ratio)
    for index in range(extent_a):
        third = jnp.concatenate([third_ref[part, index, 8 : 8 + extent_b, :] for part in range(2)], axis=1)
        high, low = split_value(third)
        third = product(high, matrix_ref[:, 3 * wide : 4 * wide]) + (
            product(low, matrix_ref[:, 3 * wide : 4 * wide]) + product(high, matrix_ref[:, 4 * wide : 5 * wide])
        )
        for part in range(2):
            at = slice(part * lanes, (part + 1) * lanes)
            total = difference(lambda offset: flux_ref[part, index + 4 + offset, 8 : 8 + extent_b, :])
            total = total + difference(lambda offset: side_ref[part, index, 8 + offset : 8 + offset + extent_b, :])
            out_ref[index, :, at] = local_ref[part, index, 8 : 8 + extent_b, :] + 0.2 * (total + third[:, at])


def tail(mine, other, rows):
    _, window, half, lanes = mine.shape
    extent_a, extent_b = 2 * rows, 4 * half
    wide_a, wide_b = extent_a + 16, extent_b + 16
    points = wide_a * wide_b * 2 * lanes
    scratch = lambda *shape: pltpu.VMEM(shape, jnp.float32)
    return pl.pallas_call(
        tail_kernel,
        out_shape=jax.ShapeDtypeStruct((extent_a, extent_b, 2 * lanes), jnp.float32),
        in_specs=[pl.BlockSpec(memory_space=pltpu.VMEM)] * 3,
        out_specs=pl.BlockSpec(memory_space=pltpu.VMEM),
        scratch_shapes=[
            scratch(window, 4 * half, lanes),
            scratch(wide_a, 4 * half, lanes),
            scratch(wide_a, wide_b, lanes),
            scratch(2, wide_a, wide_b, lanes),
            scratch(2, extent_a + 8, wide_b, lanes),
            scratch(2, extent_a + 8, wide_b, lanes),
            scratch(2, extent_a, wide_b, lanes),
            scratch(2, extent_a, wide_b, lanes),
            scratch(2, extent_a, wide_b, lanes),
        ],
        compiler_params=pltpu.CompilerParams(vmem_limit_bytes=VMEM_LIMIT),
        cost_estimate=pl.CostEstimate(
            flops=100 * points, bytes_accessed=8 * points, transcendentals=2 * points
        ),
    )(mine, other, jnp.asarray(third_matrices(lanes)))


def on_device(orbitals, occupations):
    devices, domains = lax.axis_size("band"), lax.axis_size("dom")
    bands, layers, columns, lanes = orbitals.shape
    rows, half, planes = layers // devices, columns // 2, devices // 4
    place = lax.axis_index("band")
    core, side = lax.rem(place, 2), lax.rem(lax.div(place, 2), 2)
    scale = 1.0 / (bands * devices)
    swap_cores = [(i, i ^ 1) for i in range(devices)]

    send = partial_density(orbitals, occupations, scale, True)
    other = lax.ppermute(send, "band", swap_cores)
    keep = partial_density(orbitals, occupations, scale, False)
    total, *sends = combine(keep, other, planes)
    for step, value in enumerate(sends, 1):
        total = total + lax.ppermute(value, "band", [(i, (i + 4 * step) % devices) for i in range(devices)])

    def to(turn, move):
        pairs = []
        for i in range(devices):
            for j in range(domains):
                there = (j + (1 if i % 2 else -1)) % domains if move else j
                pairs.append((i * domains + j, (i ^ turn) * domains + there))
        return pairs

    both = ("band", "dom")
    window = 2 * rows + BEFORE + AFTER
    mine = lax.dynamic_slice_in_dim(total, 2 * rows * side, window, 0)
    theirs = lax.dynamic_slice_in_dim(total, 2 * rows * (1 - side), window, 0)
    own = mine + lax.ppermute(theirs, both, to(2, False))
    beside = lax.ppermute(mine, both, to(0, True)) + lax.ppermute(theirs, both, to(2, True))
    blocks = jnp.stack([own, beside])
    window = rows + BEFORE + AFTER
    mine = lax.dynamic_slice_in_dim(blocks, rows * core, window, 1)
    theirs = lax.dynamic_slice_in_dim(blocks, rows * (1 - core), window, 1)
    return tail(mine, lax.ppermute(theirs, "band", swap_cores), rows)


def solution(mesh):
    return jax.shard_map(
        on_device,
        mesh=mesh,
        in_specs=(P("band", None, "dom", None), P("band")),
        out_specs=P("band", "dom", None),
        check_vma=False,
    )
```

time: 49.2 us -> 33.8 us (0.69)
  the two profiles are of different devices: /device:TPU:0 before, /device:TPU:15 now
where the time goes in v2:
time: 33.8 us; the launch traced here: 33.6 us
  waiting for transfers between devices  16.2 us (48%)
  starting transfers between devices  9.84 us (29%)
  Pallas kernels  5.13 us (15%)
  local copies, waits for them, and re-layouts  2.26 us (7%)
    ppermute x3, waiting for transfers between devices, on_device(): lax.ppermute(value, 'band', [(i, (i + 4 * step) % devices) for i in range...  9.86 us
    ppermute x3, starting transfers between devices, on_device(): lax.ppermute(value, 'band', [(i, (i + 4 * step) % devices) for i in range...  3.83 us
    ppermute x1, starting transfers between devices, on_device(): return tail(mine, lax.ppermute(theirs, 'band', swap_cores), rows)  3.5 us
    pallas_call x1, Pallas kernels, tail(): pl.pallas_call(tail_kernel, out_shape=jax.ShapeDtypeStruct((extent_a, ext...  2.78 us
    unnamed x6, local copies, waits for them, and re-layouts  2.25 us
    pallas_call x2, Pallas kernels, partial_density(): pl.pallas_call(functools.partial(density_kernel, scale, other), out_shape...  2.13 us
    ppermute x1, waiting for transfers between devices, on_device(): lax.ppermute(theirs, both, to(2, True))  2.06 us
    ppermute x1, waiting for transfers between devices, on_device(): own = mine + lax.ppermute(theirs, both, to(2, False))  1.93 us
  transfers between devices with their start and end apart: 8, of which 8 were waited for; matrix products, arithmetic and copies ran while one was open for 0% of the time, Pallas kernels for 3%

profile of v2, /device:TPU:15, one launch (start us, length us, event | category | flops | bytes accessed | tf_op | source)
XLA Modules:
  0.0 33.6 jit_solution(6150200837662882739)
XLA Ops:
  0.0 1.6 %copy-done = bf16[8,64,16,128]{3,2,1,0:T(8,128)(2,1)S(1)} copy-done((bf16[8,64,16,128]{3,2,1,0:T(8,128)(2,1)S(1)}, bf16[8,64,16,128]{3,2,1,0:T(8,128)(2,1)}, u32[]{:S(2)}) %copy-start) | copy-done | bytes 2097176
  1.6 0.7 %copy-done.2 = f32[8]{0:T(128)S(1)} copy-done((f32[8]{0:T(128)S(1)}, f32[8]{0:T(128)}, u32[]{:S(2)}) %copy-start.2) | copy-done | bytes 56
  2.2 1.1 %shard_map.38 = f32[64,8,128]{2,1,0:T(8,128)S(1)} custom-call(f32[8]{0:T(128)S(1)} %copy-done.2, bf16[8,64,16,128]{3,2,1,0:T(8,128)(2,1)S(1)} %copy-done), custom_call_target="tpu_custom_call" | custom-call | flops 2097152 | bytes 1310720 | tf_op jit(solution)/shard_map/pallas_call | solution.py:75
  3.3 0.0 copy-start.1
  3.3 0.7 %collective-permute-start = (f32[64,8,128]{2,1,0:T(8,128)S(1)}, f32[64,8,128]{2,1,0:T(8,128)S(1)}, u32[]{:S(2)}, u32[]{:S(2)}) collective-permute-start(f32[64,8,128]{2,1,0:T(8,128)S(1)} %shard_map.38), channel_id=1, source_target_pairs={{0,2},{2,0},{4,6},{6,4},{8,10},{10,8},{12,14},{14,12},{16,18},{18,... | collective-permute-start | bytes 786440 | tf_op jit(solution)/shard_map/ppermute | solution.py:241
  4.1 1.1 %shard_map.37.keep_ref = f32[64,8,128]{2,1,0:T(8,128)S(1)} custom-call(f32[8]{0:T(128)S(1)} %copy-done.2, bf16[8,64,16,128]{3,2,1,0:T(8,128)(2,1)S(1)} %copy-done), custom_call_target="tpu_custom_call" | custom-call | flops 2097152 | bytes 1310720 | tf_op jit(solution)/shard_map/pallas_call | solution.py:75
  5.1 0.1 collective-permute-done.other_ref
  5.2 0.2 shard_map.39
  5.5 1.3 %collective-permute-start.1 = (f32[29,8,128]{2,1,0:T(8,128)S(1)}, f32[29,8,128]{2,1,0:T(8,128)S(1)}, u32[]{:S(2)}, u32[]{:S(2)}) collective-permute-start(f32[29,8,128]{2,1,0:T(8,128)S(1)} %get-tuple-element.10), channel_id=1, source_target_pairs={{0,8},{2,10},{4,12},{6,14},{8,16},{10,18},{12,20},{14,22},{16,24},... | collective-permute-start | bytes 356360 | tf_op jit(solution)/shard_map/ppermute | solution.py:245
  6.8 1.1 %collective-permute-start.2 = (f32[29,8,128]{2,1,0:T(8,128)S(1)}, f32[29,8,128]{2,1,0:T(8,128)S(1)}, u32[]{:S(2)}, u32[]{:S(2)}) collective-permute-start(f32[29,8,128]{2,1,0:T(8,128)S(1)} %get-tuple-element.11), channel_id=1, source_target_pairs={{0,16},{2,18},{4,20},{6,22},{8,24},{10,26},{12,28},{14,30},{16,0},... | collective-permute-start | bytes 356360 | tf_op jit(solution)/shard_map/ppermute | solution.py:245
  7.9 1.4 %collective-permute-start.3 = (f32[29,8,128]{2,1,0:T(8,128)S(1)}, f32[29,8,128]{2,1,0:T(8,128)S(1)}, u32[]{:S(2)}, u32[]{:S(2)}) collective-permute-start(f32[29,8,128]{2,1,0:T(8,128)S(1)} %get-tuple-element.12), channel_id=1, source_target_pairs={{0,24},{2,26},{4,28},{6,30},{8,0},{10,2},{12,4},{14,6},{16,8},{18,... | collective-permute-start | bytes 356360 | tf_op jit(solution)/shard_map/ppermute | solution.py:245
  9.3 0.6 %collective-permute-done.1 = f32[29,8,128]{2,1,0:T(8,128)S(1)} collective-permute-done((f32[29,8,128]{2,1,0:T(8,128)S(1)}, f32[29,8,128]{2,1,0:T(8,128)S(1)}, u32[]{:S(2)}, u32[]{:S(2)}) %collective-permute-start.1) | collective-permute-done | bytes 118816 | tf_op jit(solution)/shard_map/ppermute | solution.py:245
  9.9 6.7 %collective-permute-done.2 = f32[29,8,128]{2,1,0:T(8,128)S(1)} collective-permute-done((f32[29,8,128]{2,1,0:T(8,128)S(1)}, f32[29,8,128]{2,1,0:T(8,128)S(1)}, u32[]{:S(2)}, u32[]{:S(2)}) %collective-permute-start.2) | collective-permute-done | bytes 118816 | tf_op jit(solution)/shard_map/ppermute | solution.py:245
  16.7 2.5 %collective-permute-done.3 = f32[29,8,128]{2,1,0:T(8,128)S(1)} collective-permute-done((f32[29,8,128]{2,1,0:T(8,128)S(1)}, f32[29,8,128]{2,1,0:T(8,128)S(1)}, u32[]{:S(2)}, u32[]{:S(2)}) %collective-permute-start.3) | collective-permute-done | bytes 118816 | tf_op jit(solution)/shard_map/ppermute | solution.py:245
  19.2 0.3 collective-permute-start.4
  19.5 1.2 %collective-permute-start.6 = (f32[21,8,128]{2,1,0:T(8,128)S(1)}, f32[21,8,128]{2,1,0:T(8,128)S(1)}, u32[]{:S(2)}, u32[]{:S(2)}) collective-permute-start(f32[21,8,128]{2,1,0:T(8,128)S(1)} %constant_dynamic-slice_fusion), channel_id=1, source_target_pairs={{0,5},{1,4},{2,7},{3,6},{4,1},{5,0},{6,3},{7,2},{8,13},{9,12},{10,... | collective-permute-start | bytes 258056 | tf_op jit(solution)/shard_map/ppermute | solution.py:260
  20.7 1.9 %collective-permute-done.4 = f32[21,8,128]{2,1,0:T(8,128)S(1)} collective-permute-done((f32[21,8,128]{2,1,0:T(8,128)S(1)}, f32[21,8,128]{2,1,0:T(8,128)S(1)}, u32[]{:S(2)}, u32[]{:S(2)}) %collective-permute-start.4) | collective-permute-done | bytes 86048 | tf_op jit(solution)/shard_map/ppermute | solution.py:259
  22.6 0.3 collective-permute-start.5
  22.9 2.1 %collective-permute-done.6 = f32[21,8,128]{2,1,0:T(8,128)S(1)} collective-permute-done((f32[21,8,128]{2,1,0:T(8,128)S(1)}, f32[21,8,128]{2,1,0:T(8,128)S(1)}, u32[]{:S(2)}, u32[]{:S(2)}) %collective-permute-start.6) | collective-permute-done | bytes 86048 | tf_op jit(solution)/shard_map/ppermute | solution.py:260
  25.0 1.3 %collective-permute-done.5 = f32[21,8,128]{2,1,0:T(8,128)S(1)} collective-permute-done((f32[21,8,128]{2,1,0:T(8,128)S(1)}, f32[21,8,128]{2,1,0:T(8,128)S(1)}, u32[]{:S(2)}, u32[]{:S(2)}) %collective-permute-start.5) | collective-permute-done | bytes 86048 | tf_op jit(solution)/shard_map/ppermute | solution.py:260
  26.3 3.5 %collective-permute-start.7 = (f32[2,17,8,128]{3,2,1,0:T(8,128)S(1)}, f32[2,17,8,128]{3,2,1,0:T(8,128)S(1)}, u32[]{:S(2)}, u32[]{:S(2)}) collective-permute-start(f32[2,17,8,128]{3,2,1,0:T(8,128)S(1)} %get-tuple-element.15), channel_id=1, source_target_pairs={{0,2},{2,0},{4,6},{6,4},{8,10},{10,8},{12,14},{14,12},{16,18},{18,... | collective-permute-start | bytes 417800 | tf_op jit(solution)/shard_map/ppermute | solution.py:265
  29.8 1.0 %collective-permute-done.7.other_ref = f32[2,17,8,128]{3,2,1,0:T(8,128)S(1)} collective-permute-done((f32[2,17,8,128]{3,2,1,0:T(8,128)S(1)}, f32[2,17,8,128]{3,2,1,0:T(8,128)S(1)}, u32[]{:S(2)}, u32[]{:S(2)}) %collective-permute-start.7) | collective-permute-done | bytes 139296 | tf_op jit(solution)/shard_map/ppermute | solution.py:265
  30.8 0.0 copy-done.1
  30.8 2.8 %shard_map.40 = f32[8,32,256]{2,1,0:T(8,128)} custom-call(f32[2,17,8,128]{3,2,1,0:T(8,128)S(1)} %get-tuple-element.16.mine_ref, f32[2,17,8,128]{3,2,1,0:T(8,128)S(1)} %collective-permute-done.7.other_ref, bf16[256,1280]{1,0:T(8,128)(2,1)S(1)} %copy-done.1), custom_call_target="tpu_custom_call" | custom-call | flops 29491200 | bytes 2359296 | tf_op jit(solution)/shard_map/pallas_call | solution.py:208
  (7 shorter events, 0.1 us)
Async XLA Ops:
  0.0 1.6 %copy-start = (bf16[8,64,16,128]{3,2,1,0:T(8,128)(2,1)S(1)}, bf16[8,64,16,128]{3,2,1,0:T(8,128)(2,1)}, u32[]{:S(2)}) copy-start(bf16[8,64,16,128]{3,2,1,0:T(8,128)(2,1)} %orbitals_ref.3) | copy-start | bytes 6291460
  1.6 0.7 %copy-start.2 = (f32[8]{0:T(128)S(1)}, f32[8]{0:T(128)}, u32[]{:S(2)}) copy-start(f32[8]{0:T(128)} %occupations_ref.3) | copy-start | bytes 100
  3.3 27.5 %copy-start.1 = (bf16[256,1280]{1,0:T(8,128)(2,1)S(1)}, bf16[256,1280]{1,0:T(8,128)(2,1)}, u32[]{:S(2)}) copy-start(bf16[256,1280]{1,0:T(8,128)(2,1)} %constant.27.clone.matrix_ref) | copy-start | bytes 1966084
  3.3 1.9 %collective-permute-start = (f32[64,8,128]{2,1,0:T(8,128)S(1)}, f32[64,8,128]{2,1,0:T(8,128)S(1)}, u32[]{:S(2)}, u32[]{:S(2)}) collective-permute-start(f32[64,8,128]{2,1,0:T(8,128)S(1)} %shard_map.38), channel_id=1, source_target_pairs={{0,2},{2,0},{4,6},{6,4},{8,10},{10,8},{12,14},{14,12},{16,18},{18,... | collective-permute-start | bytes 786440 | tf_op jit(solution)/shard_map/ppermute | solution.py:241
  5.5 4.5 %collective-permute-start.1 = (f32[29,8,128]{2,1,0:T(8,128)S(1)}, f32[29,8,128]{2,1,0:T(8,128)S(1)}, u32[]{:S(2)}, u32[]{:S(2)}) collective-permute-start(f32[29,8,128]{2,1,0:T(8,128)S(1)} %get-tuple-element.10), channel_id=1, source_target_pairs={{0,8},{2,10},{4,12},{6,14},{8,16},{10,18},{12,20},{14,22},{16,24},... | collective-permute-start | bytes 356360 | tf_op jit(solution)/shard_map/ppermute | solution.py:245
  6.8 9.9 %collective-permute-start.2 = (f32[29,8,128]{2,1,0:T(8,128)S(1)}, f32[29,8,128]{2,1,0:T(8,128)S(1)}, u32[]{:S(2)}, u32[]{:S(2)}) collective-permute-start(f32[29,8,128]{2,1,0:T(8,128)S(1)} %get-tuple-element.11), channel_id=1, source_target_pairs={{0,16},{2,18},{4,20},{6,22},{8,24},{10,26},{12,28},{14,30},{16,0},... | collective-permute-start | bytes 356360 | tf_op jit(solution)/shard_map/ppermute | solution.py:245
  7.9 11.3 %collective-permute-start.3 = (f32[29,8,128]{2,1,0:T(8,128)S(1)}, f32[29,8,128]{2,1,0:T(8,128)S(1)}, u32[]{:S(2)}, u32[]{:S(2)}) collective-permute-start(f32[29,8,128]{2,1,0:T(8,128)S(1)} %get-tuple-element.12), channel_id=1, source_target_pairs={{0,24},{2,26},{4,28},{6,30},{8,0},{10,2},{12,4},{14,6},{16,8},{18,... | collective-permute-start | bytes 356360 | tf_op jit(solution)/shard_map/ppermute | solution.py:245
  19.2 3.4 %collective-permute-start.4 = (f32[21,8,128]{2,1,0:T(8,128)S(1)}, f32[21,8,128]{2,1,0:T(8,128)S(1)}, u32[]{:S(2)}, u32[]{:S(2)}) collective-permute-start(f32[21,8,128]{2,1,0:T(8,128)S(1)} %constant_dynamic-slice_fusion), channel_id=1, source_target_pairs={{0,4},{1,5},{2,6},{3,7},{4,0},{5,1},{6,2},{7,3},{8,12},{9,13},{10,... | collective-permute-start | bytes 258056 | tf_op jit(solution)/shard_map/ppermute | solution.py:259
  19.5 5.5 %collective-permute-start.6 = (f32[21,8,128]{2,1,0:T(8,128)S(1)}, f32[21,8,128]{2,1,0:T(8,128)S(1)}, u32[]{:S(2)}, u32[]{:S(2)}) collective-permute-start(f32[21,8,128]{2,1,0:T(8,128)S(1)} %constant_dynamic-slice_fusion), channel_id=1, source_target_pairs={{0,5},{1,4},{2,7},{3,6},{4,1},{5,0},{6,3},{7,2},{8,13},{9,12},{10,... | collective-permute-start | bytes 258056 | tf_op jit(solution)/shard_map/ppermute | solution.py:260
  22.6 3.6 %collective-permute-start.5 = (f32[21,8,128]{2,1,0:T(8,128)S(1)}, f32[21,8,128]{2,1,0:T(8,128)S(1)}, u32[]{:S(2)}, u32[]{:S(2)}) collective-permute-start(f32[21,8,128]{2,1,0:T(8,128)S(1)} %get-tuple-element.14), channel_id=1, source_target_pairs={{0,1},{1,0},{2,3},{3,2},{4,5},{5,4},{6,7},{7,6},{8,9},{9,8},{10,11... | collective-permute-start | bytes 258056 | tf_op jit(solution)/shard_map/ppermute | solution.py:260
  26.3 4.5 %collective-permute-start.7 = (f32[2,17,8,128]{3,2,1,0:T(8,128)S(1)}, f32[2,17,8,128]{3,2,1,0:T(8,128)S(1)}, u32[]{:S(2)}, u32[]{:S(2)}) collective-permute-start(f32[2,17,8,128]{3,2,1,0:T(8,128)S(1)} %get-tuple-element.15), channel_id=1, source_target_pairs={{0,2},{2,0},{4,6},{6,4},{8,10},{10,8},{12,14},{14,12},{16,18},{18,... | collective-permute-start | bytes 417800 | tf_op jit(solution)/shard_map/ppermute | solution.py:265

commit v3 on v2

--- a/solution.py
+++ b/solution.py
@@ -44,45 +44,84 @@
     return np.concatenate([twice(refine).astype(bf16), *both, *split_matrix(derive)], axis=1)
 
 
-def density_kernel(scale, other, occupations_ref, orbitals_ref, out_ref, buffer_ref, sems):
+def band_sum(weight, values_ref, rows):
+    total = None
+    for band in range(values_ref.shape[0]):
+        value = values_ref[band, rows].astype(jnp.float32)
+        term = weight(band) * (value * value)
+        total = term if total is None else total + term
+    return total
+
+
+def send_kernel(scale, occupations_ref, orbitals_ref, out_ref, held_ref, spread_ref, buffer_ref, weights_ref, sems, weights_sem, held_sem):
     bands, layers, half, _ = buffer_ref.shape
     core = lax.rem(lax.axis_index("band"), 2)
-    start = pl.multiple_of((1 - core if other else core) * half, half)
+    columns = lambda which: pl.ds(pl.multiple_of(which * half, half), half)
+    weights_copy = pltpu.make_async_copy(occupations_ref, weights_ref, weights_sem)
+    weights_copy.start()
     chunk = layers // sems.shape[0]
     copies = []
     for index in range(sems.shape[0]):
         rows = pl.ds(index * chunk, chunk)
         copy = pltpu.make_async_copy(
-            orbitals_ref.at[:, rows, pl.ds(start, half), :], buffer_ref.at[:, rows], sems.at[index]
+            orbitals_ref.at[:, rows, columns(1 - core), :], buffer_ref.at[:, rows], sems.at[index]
         )
         copy.start()
         copies.append(copy)
+    held_copy = pltpu.make_async_copy(orbitals_ref.at[:, :, columns(core), :], held_ref, held_sem)
+    held_copy.start()
+    weights_copy.wait()
+    for band in range(bands):
+        spread_ref[band] = jnp.full(spread_ref.shape[1:], weights_ref[band] * scale, jnp.float32)
     for index, copy in enumerate(copies):
         copy.wait()
         rows = slice(index * chunk, (index + 1) * chunk)
-        total = None
-        for band in range(bands):
-            value = buffer_ref[band, rows].astype(jnp.float32)
-            term = (occupations_ref[band] * scale) * (value * value)
-            total = term if total is None else total + term
-        out_ref[rows] = total
-
-
-def partial_density(orbitals, occupations, scale, other):
+        out_ref[rows] = band_sum(lambda band: weights_ref[band] * scale, buffer_ref, rows)
+    held_copy.wait()
+
+
+def keep_kernel(held_ref, spread_ref, out_ref):
+    layers = out_ref.shape[0]
+    for start in range(0, layers, 16):
+        rows = slice(start, min(start + 16, layers))
+        out_ref[rows] = band_sum(lambda band: spread_ref[band], held_ref, rows)
+
+
+def partial_densities(orbitals, occupations, scale):
     bands, layers, columns, lanes = orbitals.shape
     half = columns // 2
     points = layers * half * lanes
-    return pl.pallas_call(
-        functools.partial(density_kernel, scale, other),
-        out_shape=jax.ShapeDtypeStruct((layers, half, lanes), jnp.float32),
-        in_specs=[pl.BlockSpec(memory_space=pltpu.SMEM), pl.BlockSpec(memory_space=pl.ANY)],
-        out_specs=pl.BlockSpec(memory_space=pltpu.VMEM),
-        scratch_shapes=[pltpu.VMEM((bands, layers, half, lanes), orbitals.dtype), pltpu.SemaphoreType.DMA((4,))],
-        compiler_params=pltpu.CompilerParams(vmem_limit_bytes=VMEM_LIMIT),
-        cost_estimate=pl.CostEstimate(
-            flops=4 * bands * points, bytes_accessed=(2 * bands + 4) * points, transcendentals=0
-        ),
-    )(occupations, orbitals)
+    density = jax.ShapeDtypeStruct((layers, half, lanes), jnp.float32)
+    held = jax.ShapeDtypeStruct((bands, layers, half, lanes), orbitals.dtype)
+    spread = jax.ShapeDtypeStruct((bands, half, lanes), jnp.float32)
+    in_vmem = pl.BlockSpec(memory_space=pltpu.VMEM)
+    in_hbm = lambda value: pltpu.with_memory_space_constraint(value, pltpu.MemorySpace.HBM)
+    params = pltpu.CompilerParams(vmem_limit_bytes=VMEM_LIMIT)
+    cost = pl.CostEstimate(flops=4 * bands * points, bytes_accessed=4 * bands * points, transcendentals=0)
+    send, held, spread = pl.pallas_call(
+        functools.partial(send_kernel, scale),
+        out_shape=[density, held, spread],
+        in_specs=[pl.BlockSpec(memory_space=pltpu.MemorySpace.HBM)] * 2,
+        out_specs=[in_vmem] * 3,
+        scratch_shapes=[
+            pltpu.VMEM(held.shape, held.dtype),
+            pltpu.SMEM((bands,), jnp.float32),
+            pltpu.SemaphoreType.DMA((4,)),
+            pltpu.SemaphoreType.DMA,
+            pltpu.SemaphoreType.DMA,
+        ],
+        compiler_params=params,
+        cost_estimate=cost,
+    )(in_hbm(occupations), in_hbm(orbitals))
+    keep = lambda: pl.pallas_call(
+        keep_kernel,
+        out_shape=density,
+        in_specs=[in_vmem] * 2,
+        out_specs=in_vmem,
+        compiler_params=params,
+        cost_estimate=cost,
+    )(held, spread)
+    return send, keep
 
 
 def combine_kernel(planes, keep_ref, other_ref, *out_refs):
@@ -237,12 +276,16 @@
     scale = 1.0 / (bands * devices)
     swap_cores = [(i, i ^ 1) for i in range(devices)]
 
-    send = partial_density(orbitals, occupations, scale, True)
+    send, keep = partial_densities(orbitals, occupations, scale)
     other = lax.ppermute(send, "band", swap_cores)
-    keep = partial_density(orbitals, occupations, scale, False)
-    total, *sends = combine(keep, other, planes)
-    for step, value in enumerate(sends, 1):
-        total = total + lax.ppermute(value, "band", [(i, (i + 4 * step) % devices) for i in range(devices)])
+    total, *sends = combine(keep(), other, planes)
+    received = [None] * planes
+    for step in sorted(range(1, planes), key=lambda step: abs(2 * step - planes)):
+        received[step] = lax.ppermute(
+            sends[step - 1], "band", [(i, (i + 4 * step) % devices) for i in range(devices)]
+        )
+    for value in received[1:]:
+        total = total + value
 
     def to(turn, move):
         pairs = []
@@ -256,6 +299,7 @@
     window = 2 * rows + BEFORE + AFTER
     mine = lax.dynamic_slice_in_dim(total, 2 * rows * side, window, 0)
     theirs = lax.dynamic_slice_in_dim(total, 2 * rows * (1 - side), window, 0)
+    mine, theirs = lax.optimization_barrier((mine, theirs))
     own = mine + lax.ppermute(theirs, both, to(2, False))
     beside = lax.ppermute(mine, both, to(0, True)) + lax.ppermute(theirs, both, to(2, True))
     blocks = jnp.stack([own, beside])

time: 33.8 us -> 30.7 us (0.908)
  the two profiles are of different devices: /device:TPU:15 before, /device:TPU:0 now
where the time goes in v3:
time: 30.7 us; the launch traced here: 30.2 us
  waiting for transfers between devices  14 us (46%)
  starting transfers between devices  11.1 us (36%)
  Pallas kernels  4.86 us (16%)
    ppermute x3, starting transfers between devices, on_device(): lax.ppermute(sends[step - 1], 'band', [(i, (i + 4 * step) % devices) for...  6.92 us
    ppermute x3, waiting for transfers between devices, on_device(): lax.ppermute(sends[step - 1], 'band', [(i, (i + 4 * step) % devices) for...  6.81 us
    ppermute x1, waiting for transfers between devices, on_device(): lax.ppermute(mine, both, to(0, True))  3.97 us
    pallas_call x1, Pallas kernels, tail(): pl.pallas_call(tail_kernel, out_shape=jax.ShapeDtypeStruct((extent_a, ext...  2.78 us
    pallas_call x1, Pallas kernels, partial_densities(): pl.pallas_call(functools.partial(send_kernel, scale), out_shape=[density,...  1.6 us
    ppermute x1, starting transfers between devices, on_device(): own = mine + lax.ppermute(theirs, both, to(2, False))  1.56 us
    ppermute x1, starting transfers between devices, on_device(): lax.ppermute(theirs, both, to(2, True))  1.49 us
    ppermute x1, waiting for transfers between devices, on_device(): return tail(mine, lax.ppermute(theirs, 'band', swap_cores), rows)  1.35 us
  transfers between devices with their start and end apart: 8, of which 6 were waited for; matrix products, arithmetic and copies ran while one was open for 0% of the time, Pallas kernels for 1%

profile of v3, /device:TPU:0, one launch (start us, length us, event | category | flops | bytes accessed | tf_op | source)
XLA Modules:
  0.0 30.2 jit_solution(8987308641356783327)
XLA Ops:
  0.0 1.6 %shard_map.37 = (f32[64,8,128]{2,1,0:T(8,128)S(1)}, bf16[8,64,8,128]{3,2,1,0:T(8,128)(2,1)S(1)}, f32[8,8,128]{2,1,0:T(8,128)S(1)}) custom-call(f32[8]{0:T(128)} %occupations_ref.1, bf16[8,64,16,128]{3,2,1,0:T(8,128)(2,1)} %orbitals_ref.1), custom_call_target="tpu_custom_call" | custom-call | flops 2097152 | bytes 2097152 | tf_op jit(solution)/shard_map/pallas_call | solution.py:101
  1.6 0.0 copy-start
  1.6 0.6 %collective-permute-start = (f32[64,8,128]{2,1,0:T(8,128)S(1)}, f32[64,8,128]{2,1,0:T(8,128)S(1)}, u32[]{:S(2)}, u32[]{:S(2)}) collective-permute-start(f32[64,8,128]{2,1,0:T(8,128)S(1)} %get-tuple-element.16), channel_id=1, source_target_pairs={{0,2},{2,0},{4,6},{6,4},{8,10},{10,8},{12,14},{14,12},{16,18},{18,... | collective-permute-start | bytes 786440 | tf_op jit(solution)/shard_map/ppermute | solution.py:280
  2.2 0.3 shard_map.38.keep_ref
  2.5 0.9 %collective-permute-done.other_ref = f32[64,8,128]{2,1,0:T(8,128)S(1)} collective-permute-done((f32[64,8,128]{2,1,0:T(8,128)S(1)}, f32[64,8,128]{2,1,0:T(8,128)S(1)}, u32[]{:S(2)}, u32[]{:S(2)}) %collective-permute-start) | collective-permute-done | bytes 262176 | tf_op jit(solution)/shard_map/ppermute | solution.py:280
  3.3 0.2 shard_map.39
  3.6 3.0 %collective-permute-start.1 = (f32[29,8,128]{2,1,0:T(8,128)S(1)}, f32[29,8,128]{2,1,0:T(8,128)S(1)}, u32[]{:S(2)}, u32[]{:S(2)}) collective-permute-start(f32[29,8,128]{2,1,0:T(8,128)S(1)} %get-tuple-element.18), channel_id=1, source_target_pairs={{0,8},{2,10},{4,12},{6,14},{8,16},{10,18},{12,20},{14,22},{16,24},... | collective-permute-start | bytes 356360 | tf_op jit(solution)/shard_map/ppermute | solution.py:284
  6.6 2.6 %collective-permute-start.2 = (f32[29,8,128]{2,1,0:T(8,128)S(1)}, f32[29,8,128]{2,1,0:T(8,128)S(1)}, u32[]{:S(2)}, u32[]{:S(2)}) collective-permute-start(f32[29,8,128]{2,1,0:T(8,128)S(1)} %get-tuple-element.19), channel_id=1, source_target_pairs={{0,16},{2,18},{4,20},{6,22},{8,24},{10,26},{12,28},{14,30},{16,0},... | collective-permute-start | bytes 356360 | tf_op jit(solution)/shard_map/ppermute | solution.py:284
  9.1 1.3 %collective-permute-start.3 = (f32[29,8,128]{2,1,0:T(8,128)S(1)}, f32[29,8,128]{2,1,0:T(8,128)S(1)}, u32[]{:S(2)}, u32[]{:S(2)}) collective-permute-start(f32[29,8,128]{2,1,0:T(8,128)S(1)} %get-tuple-element.20), channel_id=1, source_target_pairs={{0,24},{2,26},{4,28},{6,30},{8,0},{10,2},{12,4},{14,6},{16,8},{18,... | collective-permute-start | bytes 356360 | tf_op jit(solution)/shard_map/ppermute | solution.py:284
  10.5 2.3 %collective-permute-done.1 = f32[29,8,128]{2,1,0:T(8,128)S(1)} collective-permute-done((f32[29,8,128]{2,1,0:T(8,128)S(1)}, f32[29,8,128]{2,1,0:T(8,128)S(1)}, u32[]{:S(2)}, u32[]{:S(2)}) %collective-permute-start.1) | collective-permute-done | bytes 118816 | tf_op jit(solution)/shard_map/ppermute | solution.py:284
  12.8 4.5 %collective-permute-done.2 = f32[29,8,128]{2,1,0:T(8,128)S(1)} collective-permute-done((f32[29,8,128]{2,1,0:T(8,128)S(1)}, f32[29,8,128]{2,1,0:T(8,128)S(1)}, u32[]{:S(2)}, u32[]{:S(2)}) %collective-permute-start.2) | collective-permute-done | bytes 118816 | tf_op jit(solution)/shard_map/ppermute | solution.py:284
  17.3 0.0 collective-permute-done.3
  17.4 1.6 %collective-permute-start.4 = (f32[21,8,128]{2,1,0:T(8,128)S(1)}, f32[21,8,128]{2,1,0:T(8,128)S(1)}, u32[]{:S(2)}, u32[]{:S(2)}) collective-permute-start(f32[21,8,128]{2,1,0:T(8,128)S(1)} %get-tuple-element.22), channel_id=1, source_target_pairs={{0,4},{1,5},{2,6},{3,7},{4,0},{5,1},{6,2},{7,3},{8,12},{9,13},{10,... | collective-permute-start | bytes 258056 | tf_op jit(solution)/shard_map/ppermute | solution.py:303
  18.9 1.5 %collective-permute-start.6 = (f32[21,8,128]{2,1,0:T(8,128)S(1)}, f32[21,8,128]{2,1,0:T(8,128)S(1)}, u32[]{:S(2)}, u32[]{:S(2)}) collective-permute-start(f32[21,8,128]{2,1,0:T(8,128)S(1)} %get-tuple-element.22), channel_id=1, source_target_pairs={{0,5},{1,4},{2,7},{3,6},{4,1},{5,0},{6,3},{7,2},{8,13},{9,12},{10,... | collective-permute-start | bytes 258056 | tf_op jit(solution)/shard_map/ppermute | solution.py:304
  20.4 0.5 %collective-permute-start.5 = (f32[21,8,128]{2,1,0:T(8,128)S(1)}, f32[21,8,128]{2,1,0:T(8,128)S(1)}, u32[]{:S(2)}, u32[]{:S(2)}) collective-permute-start(f32[21,8,128]{2,1,0:T(8,128)S(1)} %get-tuple-element.21), channel_id=1, source_target_pairs={{0,1},{1,0},{2,3},{3,2},{4,5},{5,4},{6,7},{7,6},{8,9},{9,8},{10,11... | collective-permute-start | bytes 258056 | tf_op jit(solution)/shard_map/ppermute | solution.py:304
  20.9 1.0 %collective-permute-done.4 = f32[21,8,128]{2,1,0:T(8,128)S(1)} collective-permute-done((f32[21,8,128]{2,1,0:T(8,128)S(1)}, f32[21,8,128]{2,1,0:T(8,128)S(1)}, u32[]{:S(2)}, u32[]{:S(2)}) %collective-permute-start.4) | collective-permute-done | bytes 86048 | tf_op jit(solution)/shard_map/ppermute | solution.py:303
  21.9 4.0 %collective-permute-done.5 = f32[21,8,128]{2,1,0:T(8,128)S(1)} collective-permute-done((f32[21,8,128]{2,1,0:T(8,128)S(1)}, f32[21,8,128]{2,1,0:T(8,128)S(1)}, u32[]{:S(2)}, u32[]{:S(2)}) %collective-permute-start.5) | collective-permute-done | bytes 86048 | tf_op jit(solution)/shard_map/ppermute | solution.py:304
  25.9 0.0 collective-permute-done.6
  26.0 0.1 collective-permute-start.7
  26.0 1.3 %collective-permute-done.7.other_ref = f32[2,17,8,128]{3,2,1,0:T(8,128)S(1)} collective-permute-done((f32[2,17,8,128]{3,2,1,0:T(8,128)S(1)}, f32[2,17,8,128]{3,2,1,0:T(8,128)S(1)}, u32[]{:S(2)}, u32[]{:S(2)}) %collective-permute-start.7) | collective-permute-done | bytes 139296 | tf_op jit(solution)/shard_map/ppermute | solution.py:309
  27.4 0.0 copy-done
  27.4 2.8 %shard_map.40 = f32[8,32,256]{2,1,0:T(8,128)} custom-call(f32[2,17,8,128]{3,2,1,0:T(8,128)S(1)} %get-tuple-element.24.mine_ref, f32[2,17,8,128]{3,2,1,0:T(8,128)S(1)} %collective-permute-done.7.other_ref, bf16[256,1280]{1,0:T(8,128)(2,1)S(1)} %copy-done), custom_call_target="tpu_custom_call" | custom-call | flops 29491200 | bytes 2359296 | tf_op jit(solution)/shard_map/pallas_call | solution.py:247
  (5 shorter events, 0.1 us)
Async XLA Ops:
  1.6 25.8 %copy-start = (bf16[256,1280]{1,0:T(8,128)(2,1)S(1)}, bf16[256,1280]{1,0:T(8,128)(2,1)}, u32[]{:S(2)}) copy-start(bf16[256,1280]{1,0:T(8,128)(2,1)} %constant.27.clone.matrix_ref) | copy-start | bytes 1966084
  1.6 1.7 %collective-permute-start = (f32[64,8,128]{2,1,0:T(8,128)S(1)}, f32[64,8,128]{2,1,0:T(8,128)S(1)}, u32[]{:S(2)}, u32[]{:S(2)}) collective-permute-start(f32[64,8,128]{2,1,0:T(8,128)S(1)} %get-tuple-element.16), channel_id=1, source_target_pairs={{0,2},{2,0},{4,6},{6,4},{8,10},{10,8},{12,14},{14,12},{16,18},{18,... | collective-permute-start | bytes 786440 | tf_op jit(solution)/shard_map/ppermute | solution.py:280
  3.6 9.2 %collective-permute-start.1 = (f32[29,8,128]{2,1,0:T(8,128)S(1)}, f32[29,8,128]{2,1,0:T(8,128)S(1)}, u32[]{:S(2)}, u32[]{:S(2)}) collective-permute-start(f32[29,8,128]{2,1,0:T(8,128)S(1)} %get-tuple-element.18), channel_id=1, source_target_pairs={{0,8},{2,10},{4,12},{6,14},{8,16},{10,18},{12,20},{14,22},{16,24},... | collective-permute-start | bytes 356360 | tf_op jit(solution)/shard_map/ppermute | solution.py:284
  6.6 10.7 %collective-permute-start.2 = (f32[29,8,128]{2,1,0:T(8,128)S(1)}, f32[29,8,128]{2,1,0:T(8,128)S(1)}, u32[]{:S(2)}, u32[]{:S(2)}) collective-permute-start(f32[29,8,128]{2,1,0:T(8,128)S(1)} %get-tuple-element.19), channel_id=1, source_target_pairs={{0,16},{2,18},{4,20},{6,22},{8,24},{10,26},{12,28},{14,30},{16,0},... | collective-permute-start | bytes 356360 | tf_op jit(solution)/shard_map/ppermute | solution.py:284
  9.1 8.2 %collective-permute-start.3 = (f32[29,8,128]{2,1,0:T(8,128)S(1)}, f32[29,8,128]{2,1,0:T(8,128)S(1)}, u32[]{:S(2)}, u32[]{:S(2)}) collective-permute-start(f32[29,8,128]{2,1,0:T(8,128)S(1)} %get-tuple-element.20), channel_id=1, source_target_pairs={{0,24},{2,26},{4,28},{6,30},{8,0},{10,2},{12,4},{14,6},{16,8},{18,... | collective-permute-start | bytes 356360 | tf_op jit(solution)/shard_map/ppermute | solution.py:284
  17.4 4.6 %collective-permute-start.4 = (f32[21,8,128]{2,1,0:T(8,128)S(1)}, f32[21,8,128]{2,1,0:T(8,128)S(1)}, u32[]{:S(2)}, u32[]{:S(2)}) collective-permute-start(f32[21,8,128]{2,1,0:T(8,128)S(1)} %get-tuple-element.22), channel_id=1, source_target_pairs={{0,4},{1,5},{2,6},{3,7},{4,0},{5,1},{6,2},{7,3},{8,12},{9,13},{10,... | collective-permute-start | bytes 258056 | tf_op jit(solution)/shard_map/ppermute | solution.py:303
  18.9 7.0 %collective-permute-start.6 = (f32[21,8,128]{2,1,0:T(8,128)S(1)}, f32[21,8,128]{2,1,0:T(8,128)S(1)}, u32[]{:S(2)}, u32[]{:S(2)}) collective-permute-start(f32[21,8,128]{2,1,0:T(8,128)S(1)} %get-tuple-element.22), channel_id=1, source_target_pairs={{0,5},{1,4},{2,7},{3,6},{4,1},{5,0},{6,3},{7,2},{8,13},{9,12},{10,... | collective-permute-start | bytes 258056 | tf_op jit(solution)/shard_map/ppermute | solution.py:304
  20.4 5.5 %collective-permute-start.5 = (f32[21,8,128]{2,1,0:T(8,128)S(1)}, f32[21,8,128]{2,1,0:T(8,128)S(1)}, u32[]{:S(2)}, u32[]{:S(2)}) collective-permute-start(f32[21,8,128]{2,1,0:T(8,128)S(1)} %get-tuple-element.21), channel_id=1, source_target_pairs={{0,1},{1,0},{2,3},{3,2},{4,5},{5,4},{6,7},{7,6},{8,9},{9,8},{10,11... | collective-permute-start | bytes 258056 | tf_op jit(solution)/shard_map/ppermute | solution.py:304
  26.0 1.4 %collective-permute-start.7 = (f32[2,17,8,128]{3,2,1,0:T(8,128)S(1)}, f32[2,17,8,128]{3,2,1,0:T(8,128)S(1)}, u32[]{:S(2)}, u32[]{:S(2)}) collective-permute-start(f32[2,17,8,128]{3,2,1,0:T(8,128)S(1)} %get-tuple-element.23), channel_id=1, source_target_pairs={{0,2},{2,0},{4,6},{6,4},{8,10},{10,8},{12,14},{14,12},{16,18},{18,... | collective-permute-start | bytes 417800 | tf_op jit(solution)/shard_map/ppermute | solution.py:309
